TPU v7x, 32 devices: a whole 2x2x4 slice. The times are simulated.
32 devices in a mesh: dp: 8 (over y, x, core), mp: 4 (over z).
Axes of the slice: x: 2, y: 2, z: 4, core: 2. Of those that a mesh axis runs over, the one named last changes fastest.
Arguments:
- states: bfloat16 [512, 64, 256], P('dp', 'mp'), may hold values from -6 to 6
- key_embed: bfloat16 [512, 128], P('dp'), may hold values from -6 to 6
- partner: int32 [512], replicated, may hold values from 0 to 511, as said below
- mix_numer: int32 [512], P('dp'), may hold values from 1 to 15
- lengths: int32 [512], replicated, may hold values from 8 to 64
- w_qkv: bfloat16 [3, 256, 256], P(None, None, 'mp'), may hold values from -0.375 to 0.375
- w_out: bfloat16 [256, 256], P('mp'), may hold values from -0.375 to 0.375
- w_up: bfloat16 [256, 1024], P(None, 'mp'), may hold values from -0.375 to 0.375
- w_down: bfloat16 [1024, 256], P('mp'), may hold values from -0.1875 to 0.1875
- w_proj: bfloat16 [256, 128], replicated, may hold values from -0.375 to 0.375
Outputs:
- session_loss: float32 [512], P('dp')
- grad_states: float32 [512, 64, 256], P('dp', 'mp')
Inputs may be any that keep to these rules, and one draw needn't show every extreme that they name: partner is a permutation of the 512 sessions; a session and its partner lie in different aligned blocks of 64 sessions, and at most 10 sessions of one block have their partners in one same other block.
All inputs are finite; a program needn't handle non-finite values.
Results may differ from a plain program's by a relative error of at most 0.0091.
Values may be sent and summed in bfloat16 or wider, within the bound.
A program may use at most 64 MiB of HBM per device.

v0:
```python
import jax
import jax.numpy as jnp
from jax import lax
from jax.sharding import PartitionSpec as P

HD = 64


SOFTMAX_TEMP = 0.1
LN_EPS = 1e-05
NORM_EPS = 1e-06
TOP_PRECISION = lax.Precision.HIGHEST


def swap_rows(buffer):
    return lax.all_to_all(buffer, "dp", split_axis=0, concat_axis=0, tiled=True)


def local(states, key_embed, partner, mix_numer, lengths, w_qkv, w_out, w_up, w_down, w_proj):
    sessions_dev, ev_part, width = states.shape
    n_data = lax.axis_size("dp")
    capacity = (sessions_dev + n_data - 2) // (n_data - 1)
    device_index = lax.axis_index("dp")
    model_index = lax.axis_index("mp")
    all_keys = lax.all_gather(key_embed, "dp", axis=0, tiled=True)
    session_count = partner.shape[0]
    local_ids = jnp.arange(sessions_dev, dtype=jnp.int32)
    own_ids = device_index * sessions_dev + local_ids
    own_partner = lax.dynamic_slice_in_dim(partner, device_index * sessions_dev, sessions_dev)
    mixup_weight = mix_numer.astype(jnp.float32) / 16.0
    source = own_partner // sessions_dev
    earlier = local_ids[None, :] < local_ids[:, None]
    in_slot = jnp.sum(((source[:, None] == source[None, :]) & earlier).astype(jnp.int32), axis=1)
    wanted = partner[None, :] == own_ids[:, None]
    seeker = jnp.sum(
        jnp.where(wanted, jnp.arange(session_count, dtype=jnp.int32)[None, :], 0), axis=1
    )
    target = seeker // sessions_dev
    seeker_rows = partner.reshape(n_data, sessions_dev)[target]
    out_slot = jnp.sum(
        (
            (seeker_rows // sessions_dev == device_index)
            & (local_ids[None, :] < (seeker % sessions_dev)[:, None])
        ).astype(jnp.int32),
        axis=1,
    )
    row_len = ev_part * width
    outgoing = (
        jnp.zeros((n_data, capacity, row_len), jnp.bfloat16)
        .at[target, out_slot]
        .set(states.reshape(sessions_dev, row_len))
    )
    incoming = swap_rows(outgoing)
    partner_states = incoming[source, in_slot].reshape(sessions_dev, ev_part, width)
    mix_rows = mixup_weight[:, None, None]
    mixed_part = (
        mix_rows * states.astype(jnp.float32)
        + (1.0 - mix_rows) * partner_states.astype(jnp.float32)
    ).astype(jnp.bfloat16)
    own_lengths = lax.dynamic_slice_in_dim(lengths, device_index * sessions_dev, sessions_dev)
    len_mix = jnp.maximum(own_lengths, lengths[own_partner])
    qkv_full, out_full, up_full, down_full = (w_qkv, w_out, w_up, w_down)
    mixed = lax.all_gather(mixed_part, "mp", axis=1, tiled=True)
    layer_sessions = mixed.shape[0]
    events = mixed.shape[1]
    rows = layer_sessions * events
    positions = jnp.arange(events, dtype=jnp.int32)
    token_mask = (positions[None, :] < len_mix[:, None]).astype(jnp.float32)
    pool_weights = token_mask / len_mix[:, None].astype(jnp.float32)
    inputs_f = mixed.astype(jnp.float32).reshape(rows, width)
    row_mean = jnp.mean(inputs_f, axis=1, keepdims=True)
    centered = inputs_f - row_mean
    inv_std = lax.rsqrt(jnp.mean(centered * centered, axis=1, keepdims=True) + LN_EPS)
    unit_rows = centered * inv_std
    normed = unit_rows.astype(jnp.bfloat16)
    projected = jnp.einsum(
        "rd,jdf->jrf", normed, qkv_full, preferred_element_type=jnp.float32
    ).astype(jnp.bfloat16)
    inner_part = qkv_full.shape[2]
    heads_part = inner_part // HD
    query_h = projected[0].reshape(layer_sessions, events, heads_part, HD)
    key_h = projected[1].reshape(layer_sessions, events, heads_part, HD)
    value_h = projected[2].reshape(layer_sessions, events, heads_part, HD)
    score_scale = HD ** (-0.5)
    scores = (
        jnp.einsum("sthc,srhc->shtr", query_h, key_h, preferred_element_type=jnp.float32)
        * score_scale
    )
    exp_scores = jnp.exp(scores) * token_mask[:, None, None, :]
    probs = exp_scores / jnp.sum(exp_scores, axis=3, keepdims=True)
    probs_b = probs.astype(jnp.bfloat16)
    context = (
        jnp.einsum("shtr,srhc->sthc", probs_b, value_h, preferred_element_type=jnp.float32)
        .astype(jnp.bfloat16)
        .reshape(rows, inner_part)
    )
    pre_act = jnp.dot(normed, up_full, preferred_element_type=jnp.float32)
    hidden = jax.nn.gelu(pre_act).astype(jnp.bfloat16)
    branch = jnp.dot(context, out_full, preferred_element_type=jnp.float32) + jnp.dot(
        hidden, down_full, preferred_element_type=jnp.float32
    )
    pooled_branch = jnp.einsum(
        "st,std->sd",
        pool_weights,
        branch.reshape(layer_sessions, events, width),
        precision=TOP_PRECISION,
    )
    pooled_input = jnp.einsum(
        "st,std->sd",
        pool_weights,
        inputs_f.reshape(layer_sessions, events, width),
        precision=TOP_PRECISION,
    )
    pooled = lax.psum(pooled_branch, "mp") + pooled_input
    proj_f = w_proj.astype(jnp.float32)
    embed = jnp.dot(pooled, proj_f, precision=TOP_PRECISION)
    inv_norm = lax.rsqrt(jnp.sum(embed * embed, axis=1, keepdims=True) + NORM_EPS)
    unit_query_rows = embed * inv_norm
    keys_f = all_keys.astype(jnp.float32)
    unit_key_rows = keys_f * lax.rsqrt(jnp.sum(keys_f * keys_f, axis=1, keepdims=True) + NORM_EPS)
    pair_logits = (
        jnp.einsum("an,qn->aq", unit_query_rows, unit_key_rows, precision=TOP_PRECISION)
        / SOFTMAX_TEMP
    )
    exp_logits = jnp.exp(pair_logits)
    sum_exp = jnp.sum(exp_logits, axis=1)
    own_logit = jnp.take_along_axis(pair_logits, own_ids[:, None], axis=1)[:, 0]
    partner_logit = jnp.take_along_axis(pair_logits, own_partner[:, None], axis=1)[:, 0]
    session_loss = (
        jnp.log(sum_exp) - mixup_weight * own_logit - (1.0 - mixup_weight) * partner_logit
    )
    normalized_exponent = exp_logits / sum_exp[:, None]
    unit_gradient = (
        jnp.dot(normalized_exponent, unit_key_rows, precision=TOP_PRECISION)
        - mixup_weight[:, None] * unit_key_rows[own_ids]
        - (1.0 - mixup_weight)[:, None] * unit_key_rows[own_partner]
    ) / SOFTMAX_TEMP
    grad_embed = (
        unit_gradient
        - unit_query_rows * jnp.sum(unit_query_rows * unit_gradient, axis=1, keepdims=True)
    ) * inv_norm
    grad_pooled = jnp.einsum("se,de->sd", grad_embed, proj_f, precision=TOP_PRECISION)
    grad_full = grad_pooled[:, None, :] * pool_weights[:, :, None]
    grad_b = grad_full.reshape(rows, width).astype(jnp.bfloat16)
    d_hidden = jnp.einsum("rd,fd->rf", grad_b, down_full, preferred_element_type=jnp.float32)
    d_pre = jax.vjp(jax.nn.gelu, pre_act)[1](d_hidden)[0].astype(jnp.bfloat16)
    d_context = (
        jnp.einsum("rd,fd->rf", grad_b, out_full, preferred_element_type=jnp.float32)
        .astype(jnp.bfloat16)
        .reshape(layer_sessions, events, heads_part, HD)
    )
    d_value = jnp.einsum(
        "shtr,sthc->srhc", probs_b, d_context, preferred_element_type=jnp.float32
    ).astype(jnp.bfloat16)
    d_prob = jnp.einsum("sthc,srhc->shtr", d_context, value_h, preferred_element_type=jnp.float32)
    d_score = (
        probs * (d_prob - jnp.sum(probs * d_prob, axis=3, keepdims=True)) * score_scale
    ).astype(jnp.bfloat16)
    d_query = jnp.einsum(
        "shtr,srhc->sthc", d_score, key_h, preferred_element_type=jnp.float32
    ).astype(jnp.bfloat16)
    d_key = jnp.einsum(
        "shtr,sthc->srhc", d_score, query_h, preferred_element_type=jnp.float32
    ).astype(jnp.bfloat16)
    d_proj = jnp.stack([d_query, d_key, d_value]).reshape(3, rows, inner_part)
    d_normed = jnp.einsum(
        "jrf,jdf->rd", d_proj, qkv_full, preferred_element_type=jnp.float32
    ) + jnp.einsum("rf,df->rd", d_pre, up_full, preferred_element_type=jnp.float32)
    d_normed = d_normed.reshape(layer_sessions, events, width)
    unit_all = unit_rows.reshape(layer_sessions, events, width)
    inv_all = inv_std.reshape(layer_sessions, events, 1)
    event_start = model_index * ev_part
    unit_part = lax.dynamic_slice_in_dim(unit_all, event_start, ev_part, 1)
    inv_part = lax.dynamic_slice_in_dim(inv_all, event_start, ev_part, 1)
    d_full = lax.psum(d_normed, "mp")
    d_local = lax.dynamic_slice_in_dim(d_full, event_start, ev_part, 1)
    center = jnp.mean(d_local, axis=2, keepdims=True)
    along = jnp.mean(d_local * unit_part, axis=2, keepdims=True)
    d_mixed = (
        lax.dynamic_slice_in_dim(grad_full, event_start, ev_part, 1)
        + (d_local - center - unit_part * along) * inv_part
    )
    d_mixed_rows = d_mixed.reshape(sessions_dev, row_len)
    back_rows = ((1.0 - mixup_weight)[:, None] * d_mixed_rows).astype(jnp.bfloat16)
    returning = (
        jnp.zeros((n_data, capacity, row_len), jnp.bfloat16).at[source, in_slot].set(back_rows)
    )
    arrived = swap_rows(returning)
    grad_states = mixup_weight[:, None] * d_mixed_rows + arrived[target, out_slot].astype(
        jnp.float32
    )
    return (session_loss, grad_states.reshape(sessions_dev, ev_part, width))


def solution(mesh):
    placed = (
        P("dp", "mp", None),
        P("dp", None),
        P(),
        P("dp"),
        P(),
        P(None, None, "mp"),
        P("mp", None),
        P(None, "mp"),
        P("mp", None),
        P(),
    )
    return jax.shard_map(
        local, mesh=mesh, in_specs=placed, out_specs=(P("dp"), P("dp", "mp", None)), check_vma=False
    )
```

profile of v0, /device:TPU:0, one launch (start us, length us, event | category | flops | bytes accessed | tf_op | source)
XLA Modules:
  0.0 415.0 jit_solution(1312834488764694528)
XLA Ops:
  8.9 1.3 fusion.104
  11.0 1.2 copy.88
  12.3 9.7 %scatter_fusion = bf16[8,10,4096]{2,0,1:T(8,128)(2,1)S(1)} fusion(bf16[8,10,4096]{2,0,1:T(8,128)(2,1)S(1)} %broadcast.348.clone, s32[64]{0:T(128)S(1)} %get-tuple-element.15, bf16[64,4096]{1,0:T(8,128)(2,1)S(1)} %bitcast.216), kind=kCustom, calls=%fused_computation.8 | custom fusion | bytes 1573376 | tf_op jit(solution)/shard_map/scatter | solution.py:51
  22.0 1.4 copy.60
  23.4 5.2 %all-to-all-start = ((bf16[8,10,4096]{2,1,0:T(8,128)(2,1)}), bf16[8,10,4096]{2,1,0:T(8,128)(2,1)S(1)}, u32[]{:S(2)}, u32[]{:S(2)}) async-start(bf16[8,10,4096]{2,1,0:T(8,128)(2,1)} %copy.60), calls=%async_computation | async-start | bytes 2097152 | tf_op jit(solution)/shard_map/all_to_all | solution.py:16
  28.8 15.1 %all-to-all-done = bf16[8,10,4096]{2,1,0:T(8,128)(2,1)S(1)} async-done(((bf16[8,10,4096]{2,1,0:T(8,128)(2,1)}), bf16[8,10,4096]{2,1,0:T(8,128)(2,1)S(1)}, u32[]{:S(2)}, u32[]{:S(2)}) %all-to-all-start) | async-done | bytes 655392 | tf_op jit(solution)/shard_map/all_to_all | solution.py:16
  44.3 2.2 gather_fusion.2
  49.5 8.2 %all_gather.7 = bf16[512,128]{1,0:T(8,128)(2,1)S(1)} all-gather(bf16[64,128]{1,0:T(8,128)(2,1)S(1)} %copy-done.17), channel_id=1, replica_groups=mesh['dp'=8,'mp'=4] {'dp'}, dimensions={0}, use_global_device_ids=true | all-gather | bytes 147456 | tf_op jit(solution)/shard_map/all_gather | solution.py:25
  59.2 1.2 gather_fusion.3
  61.1 31.9 %all-gather.2.cloned.1.call-done = bf16[64,64,256]{2,1,0:T(8,128)(2,1)} async-done(((bf16[64,16,256]{2,1,0:T(8,128)(2,1)}), bf16[64,64,256]{2,1,0:T(8,128)(2,1)}) %all-gather.2.cloned.1.call-update) | async-done | bytes 2097168 | tf_op jit(solution)/shard_map/all_gather | solution.py:63
  93.0 2.4 convert_reduce_fusion
  95.4 2.7 broadcast_subtract_fusion
  98.2 2.5 fusion.10
  102.7 2.1 reshape.404
  104.8 2.1 reshape.403
  107.0 1.5 copy.87
  108.5 3.7 fusion.132
  112.3 5.0 %fusion.26 = (f32[64,64]{1,0:T(8,128)S(1)}, f32[64,64,64]{1,2,0:T(8,128)S(1)}) fusion(f32[64,64]{1,0:T(8,128)S(1)} %copy-done.15, bf16[64,64,64]{1,0,2:T(8,128)(2,1)S(1)} %copy-done.9, bf16[64,64,64]{1,0,2:T(8,128)(2,1)S(1)} %copy-done.7), kind=kOutput, calls=%fused_computation.48 | convolution fusion | flops 34336768 | bytes 2129920 | tf_op jit(solution)/shard_map/sthc,srhc->shtr/dot_general | solution.py:86
  117.3 1.3 fusion.44
  121.0 1.4 copy-done.4
  122.4 1.9 convolution_add_fusion.1
  124.3 2.1 fusion.133
  127.4 1.6 fusion.134
  128.9 31.4 %all-reduce.3.cloned.1.call-done = f32[64,256]{1,0:T(8,128)} async-done(((f32[64,256]{1,0:T(8,128)}), f32[64,256]{1,0:T(8,128)}) %all-reduce.3.cloned.1.call-update) | async-done | bytes 65552 | tf_op jit(solution)/shard_map/psum | solution.py:114
  162.1 1.3 multiply_reduce_fusion.3
  164.5 1.4 fusion.8
  166.0 1.6 convolution_convert_fusion
  167.5 2.8 reshape.407
  170.3 3.8 fusion.58
  174.1 3.4 fusion.45
  177.5 6.9 %fusion.49 = bf16[64,64,1,64]{1,3,0,2:T(8,128)(2,1)} fusion(f32[64,64,64]{1,2,0:T(8,128)} %fusion.58, bf16[64,64,64]{1,0,2:T(8,128)(2,1)} %reshape.404, f32[64,64,64]{1,2,0:T(8,128)} %copy-done.27, f32[64,64]{1,0:T(8,128)} %copy-done.29, f32[64,64]{1,0:T(8,128)} %fusion.80), kind=kOutput, calls=%fused_computation.64 | convolution fusion | flops 36704320 | bytes 3178496 | tf_op jit(solution)/shard_map/shtr,srhc->sthc/dot_general | solution.py:159
  184.4 7.9 %fusion.46 = bf16[64,64,1,64]{1,3,0,2:T(8,128)(2,1)} fusion(f32[64,64,64]{1,2,0:T(8,128)} %fusion.58, bf16[64,64,64]{1,0,2:T(8,128)(2,1)S(1)} %copy-done.8, f32[64,64,64]{1,2,0:T(8,128)} %copy-done.27, f32[64,64]{1,0:T(8,128)} %copy-done.29, f32[64,64]{1,0:T(8,128)} %fusion.80), kind=kOutput, calls=%fused_computation.63 | convolution fusion | flops 36704320 | bytes 3178496 | tf_op jit(solution)/shard_map/shtr,sthc->srhc/dot_general | solution.py:162
  192.2 1.9 copy.77
  194.1 1.6 stack.14
  195.8 1.9 copy.74
  197.7 1.6 stack.13
  199.3 1.9 copy.71
  201.2 1.6 stack.12
  202.8 4.1 convolution_bitcast_fusion
  207.0 7.0 %convolution_add_fusion = f32[4096,256]{1,0:T(8,128)} fusion(f32[4096,256]{1,0:T(8,128)} %convolution_bitcast_fusion, bf16[256,256]{1,0:T(8,128)(2,1)S(1)} %copy-done.11, f32[4096,256]{1,0:T(8,128)} %fusion.132, bf16[4096,256]{1,0:T(8,128)(2,1)S(1)} %fusion.8, bf16[256,256]{1,0:T(8,128)(2,1)S(1)} %copy-done), kind=kOutput, calls=%fused_computation.13 | convolution fusion | flops 1095761920 | bytes 14942208 | tf_op jit(solution)/shard_map/rf,df->rd/dot_general | solution.py:168
  214.1 154.6 %all-reduce.5.cloned.1.call-done = f32[64,64,256]{2,1,0:T(8,128)} async-done(((f32[64,64,256]{2,1,0:T(8,128)}), f32[64,64,256]{2,1,0:T(8,128)}) %all-reduce.5.cloned.1.call-update) | async-done | bytes 4194320 | tf_op jit(solution)/shard_map/psum | solution.py:175
  368.8 2.1 dynamic-slice_reduce_fusion
  370.8 2.0 multiply_add_fusion
  373.6 9.7 %scatter_fusion.1 = bf16[8,10,4096]{2,0,1:T(8,128)(2,1)S(1)} fusion(bf16[8,10,4096]{2,0,1:T(8,128)(2,1)S(1)} %broadcast.348, s32[64]{0:T(128)S(1)} %get-tuple-element.16, bf16[64,4096]{1,0:T(8,128)(2,1)S(1)} %multiply_convert_fusion.3), kind=kCustom, calls=%fused_computation.9 | custom fusion | bytes 1573376 | tf_op jit(solution)/shard_map/scatter | solution.py:186
  383.4 1.4 copy.78
  384.7 4.0 all-to-all-start.1
  391.1 13.0 %all-to-all-done.1 = bf16[8,10,4096]{2,1,0:T(8,128)(2,1)S(1)} async-done(((bf16[8,10,4096]{2,1,0:T(8,128)(2,1)}), bf16[8,10,4096]{2,1,0:T(8,128)(2,1)S(1)}, u32[]{:S(2)}, u32[]{:S(2)}) %all-to-all-start.1) | async-done | bytes 655392 | tf_op jit(solution)/shard_map/all_to_all | solution.py:16
  404.4 2.2 gather_fusion.5
  (127 shorter events, 21.4 us)
Async XLA Ops:
  7.2 113.8 %copy-start = (bf16[256,256]{1,0:T(8,128)(2,1)S(1)}, bf16[256,256]{1,0:T(8,128)(2,1)}, u32[]{:S(2)}) copy-start(bf16[256,256]{1,0:T(8,128)(2,1)} %param.20) | copy-start | bytes 393220
  22.0 6.8 %copy-start.25 = (s32[64]{0:T(128)S(1)}, s32[64]{0:T(128)}, u32[]{:S(2)}) copy-start(s32[64]{0:T(128)} %param.15) | copy-start | bytes 772
  23.4 20.6 %all-to-all-start = ((bf16[8,10,4096]{2,1,0:T(8,128)(2,1)}), bf16[8,10,4096]{2,1,0:T(8,128)(2,1)S(1)}, u32[]{:S(2)}, u32[]{:S(2)}) async-start(bf16[8,10,4096]{2,1,0:T(8,128)(2,1)} %copy.60), calls=%async_computation | async-start | bytes 2097152 | tf_op jit(solution)/shard_map/all_to_all | solution.py:16
  28.6 64.4 %all-gather.2.cloned.1.call-start = ((), (), s32[]{:S(2)}) async-start(), calls=%async_computation.2 | async-start | bytes 2621440 | tf_op jit(solution)/shard_map/all_gather | solution.py:63
  28.8 17.9 %copy-start.21 = (f32[64]{0:T(128)}, f32[64]{0:T(128)S(1)}, u32[]{:S(2)}) copy-start(f32[64]{0:T(128)S(1)} %get-tuple-element.21) | copy-start | bytes 772
  28.8 17.9 %copy-start.23 = (f32[64]{0:T(128)}, f32[64]{0:T(128)S(1)}, u32[]{:S(2)}) copy-start(f32[64]{0:T(128)S(1)} %get-tuple-element.20) | copy-start | bytes 772
  44.3 2.4 copy-start.6
  46.5 1.3 copy-start.1
  46.5 3.0 copy-start.17
  47.8 112.6 %all-reduce.3.cloned.1.call-start = ((), (), s32[]{:S(2)}) async-start(), calls=%async_computation.3 | async-start | bytes 131072 | tf_op jit(solution)/shard_map/psum | solution.py:114
  93.0 2.4 copy-start.2
  98.2 2.5 copy-start.14
  108.5 3.8 copy-start.7
  108.5 3.8 copy-start.9
  108.5 3.8 copy-start.15
  117.3 1.4 copy-start.27
  117.3 1.4 copy-start.29
  118.7 1.5 copy-start.12
  120.2 2.2 copy-start.4
  124.3 3.0 copy-start.3
  127.1 33.3 %copy-start.10 = (bf16[256,128]{1,0:T(8,128)(2,1)S(1)}, bf16[256,128]{1,0:T(8,128)(2,1)}, u32[]{:S(2)}) copy-start(bf16[256,128]{1,0:T(8,128)(2,1)} %param.21) | copy-start | bytes 196612
  127.1 241.7 %all-reduce.5.cloned.1.call-start = ((), (), s32[]{:S(2)}) async-start(), calls=%async_computation.4 | async-start | bytes 8388608 | tf_op jit(solution)/shard_map/psum | solution.py:175
  160.3 5.6 %copy-start.13 = (bf16[64,256]{1,0:T(8,128)(2,1)S(1)}, bf16[64,256]{1,0:T(8,128)(2,1)}, u32[]{:S(2)}) copy-start(bf16[64,256]{1,0:T(8,128)(2,1)} %param.18) | copy-start | bytes 98308
  162.1 1.3 copy-start.18
  170.3 3.8 copy-start.5
  170.3 3.8 copy-start.16
  170.3 3.8 copy-start.28
  170.3 3.8 copy-start.30
  177.5 6.9 %copy-start.8 = (bf16[64,64,64]{1,0,2:T(8,128)(2,1)S(1)}, bf16[64,64,64]{1,0,2:T(8,128)(2,1)}, u32[]{:S(2)}) copy-start(bf16[64,64,64]{1,0,2:T(8,128)(2,1)} %reshape.403) | copy-start | bytes 1572868
  202.8 4.1 copy-start.11
  370.8 2.6 copy-start.22
  383.4 5.4 %copy-start.20 = (s32[64,1,1]{0,2,1:T(1,128)S(1)}, s32[64,1,1]{0,2,1:T(1,128)}, u32[]{:S(2)}) copy-start(s32[64,1,1]{0,2,1:T(1,128)} %get-tuple-element.5) | copy-start | bytes 772
  383.4 7.2 %copy-start.19 = (f32[64]{0:T(128)S(1)}, f32[64]{0:T(128)}, u32[]{:S(2)}) copy-start(f32[64]{0:T(128)} %copy-done.18) | copy-start | bytes 772
  383.4 7.2 %copy-start.26 = (s32[64]{0:T(128)S(1)}, s32[64]{0:T(128)}, u32[]{:S(2)}) copy-start(s32[64]{0:T(128)} %param.15) | copy-start | bytes 772
  384.7 19.3 %all-to-all-start.1 = ((bf16[8,10,4096]{2,1,0:T(8,128)(2,1)}), bf16[8,10,4096]{2,1,0:T(8,128)(2,1)S(1)}, u32[]{:S(2)}, u32[]{:S(2)}) async-start(bf16[8,10,4096]{2,1,0:T(8,128)(2,1)} %copy.78), calls=%async_computation.1 | async-start | bytes 2097152 | tf_op jit(solution)/shard_map/all_to_all | solution.py:16
  404.4 2.4 copy-start.24
Sparse Core Ops, SparseCore 0:
  47.9 45.0 all-gather.1
  127.2 33.0 all-reduce.2
  214.1 154.6 all-reduce.4
where the time goes:
time: 422 us; the launch traced here: 415 us
  waiting for transfers between devices  246 us (58%)
  local copies, waits for them, and re-layouts  60.4 us (14%)
  matrix products  56 us (13%)
  other arithmetic  19.8 us (5%)
  between operations  14.9 us (4%)
  starting transfers between devices  9.5 us (2%)
  blocking collectives  8.24 us (2%)
    psum x1, waiting for transfers between devices, local(): d_full = lax.psum(d_normed, 'mp')  155 us
    all_gather x1, waiting for transfers between devices, local(): mixed = lax.all_gather(mixed_part, 'mp', axis=1, tiled=True)  31.9 us
    psum x1, waiting for transfers between devices, local(): pooled = lax.psum(pooled_branch, 'mp') + pooled_input  31.4 us
    all_to_all x2, waiting for transfers between devices, swap_rows(): return lax.all_to_all(buffer, 'dp', split_axis=0, concat_axis=0, tiled=True)  28.1 us
    scatter x2, local copies, waits for them, and re-layouts, local(): outgoing = jnp.zeros((n_data, capacity, row_len), jnp.bfloat16).at[target...  11.1 us
    scatter x2, local copies, waits for them, and re-layouts, local(): jnp.zeros((n_data, capacity, row_len), jnp.bfloat16).at[source, in_slot]  11.1 us
    all_to_all x2, starting transfers between devices, swap_rows(): return lax.all_to_all(buffer, 'dp', split_axis=0, concat_axis=0, tiled=True)  9.17 us
    another operation x6, local copies, waits for them, and re-layouts  8.6 us
  transfers between devices with their start and end apart: 5, of which 5 were waited for; matrix products, arithmetic and copies ran while one was open for 2% of the time, Pallas kernels for 0%

commit v1 on v0

v1 whole, which is shorter than its diff:
```python
import functools

import jax
import jax.numpy as jnp
from jax import lax
from jax.experimental import pallas as pl
from jax.experimental.pallas import tpu as pltpu
from jax.sharding import PartitionSpec as P

HD = 64
SOFTMAX_TEMP = 0.1
LN_EPS = 1e-05
NORM_EPS = 1e-06
HIGHEST = lax.Precision.HIGHEST
MESH = pl.DeviceIdType.MESH
F32 = jnp.float32
BF16 = jnp.bfloat16


def remote(src, dst, send_sem, recv_sem, device):
    return pltpu.make_async_remote_copy(
        src_ref=src,
        dst_ref=dst,
        send_sem=send_sem,
        recv_sem=recv_sem,
        device_id=device,
        device_id_type=MESH,
    )


def greet(n, mp):
    me, mz = lax.axis_index("dp"), lax.axis_index("mp")
    barrier = pltpu.get_barrier_semaphore()
    for o in range(1, n):
        pl.semaphore_signal(
            barrier, inc=1, device_id={"dp": lax.rem(me + o, n)}, device_id_type=MESH
        )
    for o in range(1, mp):
        pl.semaphore_signal(
            barrier, inc=1, device_id={"mp": lax.rem(mz + o, mp)}, device_id_type=MESH
        )
    pl.semaphore_wait(barrier, n - 1 + mp - 1)


def gather_kernel(
    n, mp, group, cap,
    send_idx, recv_code, mix_w,
    states, keys, wts,
    mixed, all_keys, all_wts,
    out_buf, in_buf, mix_buf,
    dp_s, dp_r, key_s, key_r, mp_s, mp_r, wz_s, wz_r, wg_s, wg_r,
):
    me, mz = lax.axis_index("dp"), lax.axis_index("mp")
    sessions = states.shape[0]
    chunk = sessions // mp
    piece = wts.shape[0] // group
    part = lax.rem(me, group)
    base = me - part
    rows = pl.ds(pl.multiple_of(part * piece, piece), piece)
    greet(n, mp)

    @pl.loop(0, n * cap)
    def _(j):
        out_buf[j] = states[send_idx[j]]

    pending = []
    wz = []
    for o in range(1, mp):
        c = remote(
            wts.at[rows], all_wts.at[mz, rows], wz_s.at[o], wz_r.at[o],
            {"mp": lax.rem(mz + o, mp)},
        )
        c.start()
        wz.append(c)
    dp = []
    for o in range(1, n):
        peer = lax.rem(me + o, n)
        c = remote(
            out_buf.at[pl.ds(peer * cap, cap)], in_buf.at[pl.ds(me * cap, cap)],
            dp_s.at[o], dp_r.at[o], {"dp": peer},
        )
        c.start()
        dp.append(c)
    for o in range(1, n):
        c = remote(
            keys, all_keys.at[pl.ds(pl.multiple_of(me * sessions, sessions), sessions)],
            key_s.at[o], key_r.at[o], {"dp": lax.rem(me + o, n)},
        )
        c.start()
        pending.append(c)
    all_keys[pl.ds(pl.multiple_of(me * sessions, sessions), sessions), :] = keys[...]
    for o in range(1, mp):
        wz[o - 1].wait()
        held = lax.rem(mz + mp - o, mp)
        for g in range(1, group):
            c = remote(
                all_wts.at[held, rows], all_wts.at[held, rows],
                wg_s.at[o, g], wg_r.at[o, g], {"dp": base + lax.rem(part + g, group)},
            )
            c.start()
            pending.append(c)
    all_wts[mz] = wts[...]
    for c in dp:
        c.wait()

    @pl.loop(0, sessions)
    def _(i):
        w = mix_w[i]
        mix_buf[i] = (
            w * states[i].astype(F32) + (1.0 - w) * in_buf[recv_code[i]].astype(F32)
        ).astype(BF16)

    for o in (2, 1, 3) if mp == 4 else range(1, mp):
        peer = lax.rem(mz + o, mp)
        c = remote(
            mix_buf.at[pl.ds(peer * chunk, chunk)], mixed.at[pl.ds(0, chunk), mz],
            mp_s.at[o], mp_r.at[o], {"mp": peer},
        )
        c.start()
        pending.append(c)

    @pl.loop(0, chunk)
    def _(i):
        mixed[i, mz] = mix_buf[mz * chunk + i]

    for c in pending:
        c.wait()


def return_kernel(
    n, mp, cap,
    recv_idx, send_code, mix_w,
    dmix, loss,
    grad, all_loss,
    dm_buf, ret_buf, arr_buf,
    mp_s, mp_r, ls_s, ls_r, dp_s, dp_r,
):
    me, mz = lax.axis_index("dp"), lax.axis_index("mp")
    chunk = dmix.shape[0]
    sessions = dm_buf.shape[0]
    greet(n, mp)
    mine = pl.ds(pl.multiple_of(mz * chunk, chunk), chunk)
    first = []
    for o in (2, 1, 3) if mp == 4 else range(1, mp):
        peer = lax.rem(mz + o, mp)
        c = remote(
            dmix.at[pl.ds(0, chunk), peer], dm_buf.at[mine], mp_s.at[o], mp_r.at[o], {"mp": peer}
        )
        c.start()
        first.append(c)
        c = remote(loss, all_loss.at[mine], ls_s.at[o], ls_r.at[o], {"mp": peer})
        c.start()
        first.append(c)
    all_loss[mine, :] = loss[...]

    @pl.loop(0, chunk)
    def _(i):
        dm_buf[mz * chunk + i] = dmix[i, mz]

    for c in first:
        c.wait()

    @pl.loop(0, n * cap)
    def _(j):
        i = recv_idx[j]
        ret_buf[j] = ((1.0 - mix_w[i]) * dm_buf[i].astype(F32)).astype(BF16)

    back = []
    for o in range(1, n):
        peer = lax.rem(me + o, n)
        c = remote(
            ret_buf.at[pl.ds(peer * cap, cap)], arr_buf.at[pl.ds(me * cap, cap)],
            dp_s.at[o], dp_r.at[o], {"dp": peer},
        )
        c.start()
        back.append(c)
    for c in back:
        c.wait()

    @pl.loop(0, sessions)
    def _(s):
        grad[s] = mix_w[s] * dm_buf[s].astype(F32) + arr_buf[send_code[s]].astype(F32)


def dot(a, b, ca=1, cb=0, precision=None):
    return lax.dot_general(
        a, b, (((ca,), (cb,)), ((), ())), precision=precision, preferred_element_type=F32
    )


def dot_split(a, b, cb=0):
    hi = a.astype(BF16)
    lo = (a - hi.astype(F32)).astype(BF16)
    return dot(hi, b, 1, cb) + dot(lo, b, 1, cb)


def layer_kernel(
    events, heads, per_block,
    lens,
    mixed, wts, keys, w_proj, aux,
    dmix, loss,
    wqkv, w_out, proj, probs, slope, hpool, xpool, ctx, d_hid, d_ctx, g_row,
):
    mp = wts.shape[0]
    width = mixed.shape[1]
    sessions = lens.shape[0]
    inner = heads * HD
    part = inner // mp
    ff_part = wts.shape[1] - 4 * part - width
    up0 = 4 * part
    down0 = up0 + width
    lanes = heads * events
    block_rows = per_block * events
    for m in range(mp):
        for j in range(3):
            wqkv[j * inner + m * part : j * inner + (m + 1) * part, :] = wts[
                m, j * part : (j + 1) * part, :
            ]
        w_out[m * part : (m + 1) * part, :] = wts[m, 3 * part : 4 * part, :]
    head_mask = (
        lax.broadcasted_iota(jnp.int32, (lanes, inner), 0) // events
        == lax.broadcasted_iota(jnp.int32, (lanes, inner), 1) // HD
    )
    ones_blk = (
        lax.broadcasted_iota(jnp.int32, (lanes, lanes), 0) // events
        == lax.broadcasted_iota(jnp.int32, (lanes, lanes), 1) // events
    ).astype(F32).astype(BF16)
    row_t = lax.broadcasted_iota(jnp.int32, (events, lanes), 0)
    lane_r = lax.broadcasted_iota(jnp.int32, (events, lanes), 1) % events
    row_w = lax.broadcasted_iota(jnp.int32, (events, width), 0)
    pool_row = lax.broadcasted_iota(jnp.int32, (per_block, block_rows), 0)
    pool_lane = lax.broadcasted_iota(jnp.int32, (per_block, block_rows), 1)
    zero_b = jnp.zeros((lanes, inner), BF16)
    scale = HD ** (-0.5)
    c0 = 0.7978845608028654

    def spread(v):
        return jnp.where(head_mask, jnp.concatenate([v] * heads, axis=0), zero_b)

    def fold(full):
        kept = jnp.where(head_mask, full, 0.0)
        total = kept[0:events]
        for h in range(1, heads):
            total = total + kept[h * events : (h + 1) * events]
        return total

    def normalise(x):
        mean = jnp.mean(x, axis=1, keepdims=True)
        centered = x - mean
        inv = lax.rsqrt(jnp.mean(centered * centered, axis=1, keepdims=True) + LN_EPS)
        return centered * inv, inv

    @pl.loop(0, sessions // per_block)
    def _(b):
        rows = pl.ds(pl.multiple_of(b * block_rows, block_rows), block_rows)
        srows = pl.ds(pl.multiple_of(b * per_block, per_block), per_block)
        mixed_b = mixed[rows, :]
        unit, _inv = normalise(mixed_b.astype(F32))
        normed = unit.astype(BF16)
        qkv = dot(normed, wqkv[...], 1, 1).astype(BF16)
        proj[rows, :] = qkv
        len_col = aux[srows, 1:2]
        pool_mask = jnp.where(
            (pool_lane // events == pool_row)
            & ((pool_lane % events).astype(F32) < len_col),
            1.0,
            0.0,
        ).astype(BF16)
        xpool[srows, :] = dot(pool_mask, mixed_b) / len_col
        for m in range(mp):
            pre = dot(normed, wts[m, up0 : up0 + width, :])
            sq = pre * pre
            th = jnp.tanh(c0 * (pre + 0.044715 * (sq * pre)))
            half = 0.5 * (1.0 + th)
            act = (pre * half).astype(BF16)
            cols = slice(m * ff_part, (m + 1) * ff_part)
            slope[rows, cols] = (
                half + 0.5 * pre * (1.0 - th * th) * (c0 * (1.0 + 3 * 0.044715 * sq))
            ).astype(BF16)
            hpool[srows, cols] = dot(pool_mask, act) / len_col
        for s in range(per_block):
            length = lens[b * per_block + s]
            lo = s * events
            q = qkv[lo : lo + events, 0:inner]
            k = qkv[lo : lo + events, inner : 2 * inner]
            v = qkv[lo : lo + events, 2 * inner : 3 * inner]
            e = jnp.where(lane_r < length, jnp.exp(dot(q, spread(k), 1, 1) * scale), 0.0)
            p = e / dot_split(e, ones_blk)
            probs[pl.ds(pl.multiple_of(b * block_rows + lo, events), events), :] = p
            used = jnp.where(row_t < length, p.astype(BF16).astype(F32), 0.0)
            seen = jnp.sum(used, axis=0, keepdims=True)
            ctx[pl.ds(b * per_block + s, 1), :] = dot_split(
                jnp.broadcast_to(seen, (8, lanes)), spread(v)
            )[0:1] / length.astype(F32)

    weight, len_all = aux[:, 0:1], aux[:, 1:2]
    own_id, partner_id = aux[:, 2:3], aux[:, 3:4]
    pooled = xpool[...] + dot_split(ctx[...], w_out[...])
    for m in range(mp):
        cols = slice(m * ff_part, (m + 1) * ff_part)
        pooled = pooled + dot_split(hpool[:, cols], wts[m, down0 : down0 + ff_part, :])
    embed = dot_split(pooled, w_proj[...])
    inv_norm = lax.rsqrt(jnp.sum(embed * embed, axis=1, keepdims=True) + NORM_EPS)
    unit_q = embed * inv_norm
    keys_f = keys[...].astype(F32)
    unit_k = keys_f * lax.rsqrt(jnp.sum(keys_f * keys_f, axis=1, keepdims=True) + NORM_EPS)
    logits = dot(unit_q, unit_k, 1, 1, HIGHEST) / SOFTMAX_TEMP
    exp_l = jnp.exp(logits)
    sum_l = jnp.sum(exp_l, axis=1, keepdims=True)
    ids = lax.broadcasted_iota(jnp.int32, logits.shape, 1).astype(F32)
    wanted = jnp.where(ids == own_id, weight, 0.0) + jnp.where(
        ids == partner_id, 1.0 - weight, 0.0
    )
    loss[...] = jnp.broadcast_to(
        jnp.log(sum_l) - jnp.sum(wanted * logits, axis=1, keepdims=True), loss.shape
    )
    grad_u = dot(exp_l / sum_l - wanted, unit_k, 1, 0, HIGHEST) / SOFTMAX_TEMP
    grad_e = (grad_u - unit_q * jnp.sum(unit_q * grad_u, axis=1, keepdims=True)) * inv_norm
    g = dot_split(grad_e, w_proj[...], 1) * (1.0 / len_all)
    g_row[...] = g
    g_b = g.astype(BF16)
    for m in range(mp):
        d_hid[:, m * ff_part : (m + 1) * ff_part] = dot(
            g_b, wts[m, down0 : down0 + ff_part, :], 1, 1
        )
    d_ctx[...] = dot(g_b, w_out[...], 1, 1)

    @pl.loop(0, sessions // per_block)
    def _(b):
        rows = pl.ds(pl.multiple_of(b * block_rows, block_rows), block_rows)
        for s in range(per_block):
            i = b * per_block + s
            srow = pl.ds(i, 1)
            length = lens[i]
            here = pl.ds(pl.multiple_of(b * block_rows + s * events, events), events)
            q = proj[here, 0:inner]
            k = proj[here, inner : 2 * inner]
            v = proj[here, 2 * inner : 3 * inner]
            p = probs[here, :]
            dc = jnp.broadcast_to(d_ctx[srow, :].astype(BF16), (events, inner))
            u = dot(dc, spread(v), 1, 1)
            kept = row_t < length
            d_score = jnp.where(
                kept, p * (u - dot_split(p * u, ones_blk)) * scale, 0.0
            ).astype(BF16)
            used = jnp.where(kept, p, 0.0).astype(BF16)
            proj[here, 0:inner] = dot(d_score, spread(k)).astype(BF16)
            proj[here, inner : 2 * inner] = fold(dot(d_score, q, 0, 0)).astype(BF16)
            proj[here, 2 * inner : 3 * inner] = fold(dot(used, dc, 0, 0)).astype(BF16)
            for m in range(mp):
                cols = slice(m * ff_part, (m + 1) * ff_part)
                kept_f = lax.broadcasted_iota(jnp.int32, (events, ff_part), 0) < length
                slope[here, cols] = jnp.where(
                    kept_f, slope[here, cols].astype(F32) * d_hid[srow, cols], 0.0
                ).astype(BF16)
        dn = dot(proj[rows, :], wqkv[...])
        for m in range(mp):
            cols = slice(m * ff_part, (m + 1) * ff_part)
            dn = dn + dot(slope[rows, cols], wts[m, up0 : up0 + width, :], 1, 1)
        unit, inv = normalise(mixed[rows, :].astype(F32))
        center = jnp.mean(dn, axis=1, keepdims=True)
        along = jnp.mean(dn * unit, axis=1, keepdims=True)
        body = (dn - center - unit * along) * inv
        for s in range(per_block):
            i = b * per_block + s
            here = pl.ds(pl.multiple_of(b * block_rows + s * events, events), events)
            direct = jnp.where(row_w < lens[i], g_row[pl.ds(i, 1), :], 0.0)
            dmix[here, :] = (direct + body[s * events : (s + 1) * events]).astype(BF16)


def local(states, key_embed, partner, mix_numer, lengths, w_qkv, w_out, w_up, w_down, w_proj):
    sessions, ev_part, width = states.shape
    n = lax.axis_size("dp")
    mp = lax.axis_size("mp")
    cap = (sessions + n - 2) // (n - 1)
    slots = n * cap
    me = lax.axis_index("dp")
    mz = lax.axis_index("mp")
    total = partner.shape[0]
    chunk = sessions // mp
    events = ev_part * mp
    inner_part = w_qkv.shape[2]
    inner = inner_part * mp
    heads = inner // HD
    ff_part = w_up.shape[1]
    group = 8 if n % 8 == 0 else 1

    source = partner.reshape(n, sessions) // sessions
    ids = jnp.arange(sessions, dtype=jnp.int32)
    slot = jnp.sum(
        (
            (source[:, :, None] == source[:, None, :]) & (ids[None, None, :] < ids[None, :, None])
        ).astype(jnp.int32),
        axis=2,
    )
    code = (jnp.arange(n, dtype=jnp.int32)[:, None] * cap + slot).reshape(-1)
    rel = partner - me * sessions
    slot_ids = jnp.arange(slots, dtype=jnp.int32)
    mine = (rel >= 0) & (rel < sessions)
    send_code = jnp.sum(jnp.where(rel[None, :] == ids[:, None], code[None, :], 0), axis=1)
    send_idx = jnp.sum(
        jnp.where((code[None, :] == slot_ids[:, None]) & mine[None, :], rel[None, :], 0), axis=1
    )
    own_source = lax.dynamic_slice_in_dim(source, me, 1, 0)[0]
    recv_code = own_source * cap + lax.dynamic_slice_in_dim(slot, me, 1, 0)[0]
    recv_idx = jnp.sum(
        jnp.where(recv_code[None, :] == slot_ids[:, None], ids[None, :], 0), axis=1
    )
    weight = mix_numer.astype(F32) / 16.0
    start = me * sessions + mz * chunk
    my_partner = lax.dynamic_slice_in_dim(partner, start, chunk)
    my_len = jnp.maximum(lax.dynamic_slice_in_dim(lengths, start, chunk), lengths[my_partner])
    aux = jnp.stack(
        [
            lax.dynamic_slice_in_dim(weight, mz * chunk, chunk),
            my_len.astype(F32),
            (start + jnp.arange(chunk, dtype=jnp.int32)).astype(F32),
            my_partner.astype(F32),
        ],
        axis=1,
    )
    wts = jnp.concatenate(
        [w_qkv.transpose(0, 2, 1).reshape(3 * inner_part, width), w_out, w_up, w_down], axis=0
    )
    smem = pl.BlockSpec(memory_space=pltpu.SMEM)
    vmem = pl.BlockSpec(memory_space=pltpu.VMEM)
    dma = pltpu.SemaphoreType.DMA

    mixed, all_keys, all_wts = pl.pallas_call(
        functools.partial(gather_kernel, n, mp, group, cap),
        out_shape=(
            jax.ShapeDtypeStruct((chunk, mp, ev_part, width), BF16),
            jax.ShapeDtypeStruct((total, key_embed.shape[1]), BF16),
            jax.ShapeDtypeStruct((mp,) + wts.shape, BF16),
        ),
        in_specs=[smem] * 3 + [vmem] * 3,
        out_specs=(vmem,) * 3,
        scratch_shapes=[
            pltpu.VMEM((slots, ev_part, width), BF16),
            pltpu.VMEM((slots, ev_part, width), BF16),
            pltpu.VMEM((sessions, ev_part, width), BF16),
            dma((n,)), dma((n,)), dma((n,)), dma((n,)),
            dma((mp,)), dma((mp,)), dma((mp,)), dma((mp,)),
            dma((mp, group)), dma((mp, group)),
        ],
        compiler_params=pltpu.CompilerParams(collective_id=0, has_side_effects=True),
    )(send_idx, recv_code, weight, states, key_embed, wts)

    rows = chunk * events
    per_block = min(8, chunk)
    dmix, loss = pl.pallas_call(
        functools.partial(layer_kernel, events, heads, per_block),
        out_shape=(
            jax.ShapeDtypeStruct((rows, width), BF16),
            jax.ShapeDtypeStruct((chunk, 128), F32),
        ),
        in_specs=[smem] + [vmem] * 5,
        out_specs=(vmem, vmem),
        scratch_shapes=[
            pltpu.VMEM((3 * inner, width), BF16),
            pltpu.VMEM((inner, width), BF16),
            pltpu.VMEM((rows, 3 * inner), BF16),
            pltpu.VMEM((rows, heads * events), F32),
            pltpu.VMEM((rows, mp * ff_part), BF16),
            pltpu.VMEM((chunk, mp * ff_part), F32),
            pltpu.VMEM((chunk, width), F32),
            pltpu.VMEM((chunk, inner), F32),
            pltpu.VMEM((chunk, mp * ff_part), F32),
            pltpu.VMEM((chunk, inner), F32),
            pltpu.VMEM((chunk, width), F32),
        ],
        compiler_params=pltpu.CompilerParams(vmem_limit_bytes=56 * 1024 * 1024),
    )(my_len, mixed.reshape(rows, width), all_wts, all_keys, w_proj, aux)

    grad, all_loss = pl.pallas_call(
        functools.partial(return_kernel, n, mp, cap),
        out_shape=(
            jax.ShapeDtypeStruct((sessions, ev_part, width), F32),
            jax.ShapeDtypeStruct((sessions, 128), F32),
        ),
        in_specs=[smem] * 3 + [vmem] * 2,
        out_specs=(vmem, vmem),
        scratch_shapes=[
            pltpu.VMEM((sessions, ev_part, width), BF16),
            pltpu.VMEM((slots, ev_part, width), BF16),
            pltpu.VMEM((slots, ev_part, width), BF16),
            dma((mp,)), dma((mp,)), dma((mp,)), dma((mp,)), dma((n,)), dma((n,)),
        ],
        compiler_params=pltpu.CompilerParams(collective_id=1, has_side_effects=True),
    )(recv_idx, send_code, weight, dmix.reshape(chunk, mp, ev_part, width), loss)
    return (all_loss[:, 0], grad)


def solution(mesh):
    placed = (
        P("dp", "mp", None),
        P("dp", None),
        P(),
        P("dp"),
        P(),
        P(None, None, "mp"),
        P("mp", None),
        P(None, "mp"),
        P("mp", None),
        P(),
    )
    return jax.shard_map(
        local, mesh=mesh, in_specs=placed, out_specs=(P("dp"), P("dp", "mp", None)), check_vma=False
    )
```

time: 422 us -> 98.1 us (0.23); the launches traced: 415 us -> 96.3 us
  waiting for transfers between devices: 246 us -> 0 us
  Pallas kernels: 0 us -> 81.3 us
  matrix products: 56 us -> 0 us
  local copies, waits for them, and re-layouts: 60.4 us -> 6.58 us
  between operations: 14.9 us -> 0.7 us
  other arithmetic: 19.8 us -> 7.71 us
  starting transfers between devices: 9.5 us -> 0 us
  blocking collectives: 8.24 us -> 0 us
    psum x2 -> x0, waiting for transfers between devices: 186 us -> none  [the longest x1 155 us: local(): d_full = lax.psum(d_normed, 'mp')]
    pallas_call x0 -> x3, Pallas kernels: none -> 81.3 us  [the longest x1 31.7 us: local(): pl.pallas_call(functools.partial(gather_kernel, n, mp, group, cap), out_s...]
    dot_general x18 -> x0, matrix products: 55.1 us -> none  [the longest x1 7.85 us: local(): jnp.einsum('shtr,sthc->srhc', d_score, query_h, preferred_element_type=jn...]
    all_gather x1 -> x0, waiting for transfers between devices: 31.9 us -> none  [local(): mixed = lax.all_gather(mixed_part, 'mp', axis=1, tiled=True)]
    all_to_all x2 -> x0, waiting for transfers between devices: 28.1 us -> none  [swap_rows(): return lax.all_to_all(buffer, 'dp', split_axis=0, concat_axis=0, tiled=True)]
    scatter x4 -> x0, local copies, waits for them, and re-layouts: 22.1 us -> none  [the longest x2 11.1 us: local(): outgoing = jnp.zeros((n_data, capacity, row_len), jnp.bfloat16).at[target...]
    another operation x10 -> x2, local copies, waits for them, and re-layouts: 13.5 us -> 0.75 us  [local(): jnp.stack([lax.dynamic_slice_in_dim(weight, mz * chunk, chunk), my_len.as...]
    all_to_all x2 -> x0, starting transfers between devices: 9.17 us -> none  [swap_rows(): return lax.all_to_all(buffer, 'dp', split_axis=0, concat_axis=0, tiled=True)]
  transfers between devices with their start and end apart: 5 -> 0, of which waited for: 5 -> 0; matrix products, arithmetic and copies ran while one was open for 2% -> 0% of each run, Pallas kernels for 0% -> 0%
where the time goes in v1:
time: 98.1 us; the launch traced here: 96.3 us
  Pallas kernels  81.3 us (83%)
  other arithmetic  7.71 us (8%)
  local copies, waits for them, and re-layouts  6.58 us (7%)
    pallas_call x1, Pallas kernels, local(): pl.pallas_call(functools.partial(gather_kernel, n, mp, group, cap), out_s...  31.7 us
    pallas_call x1, Pallas kernels, local(): pl.pallas_call(functools.partial(layer_kernel, events, heads, per_block),...  24.9 us
    pallas_call x1, Pallas kernels, local(): pl.pallas_call(functools.partial(return_kernel, n, mp, cap), out_shape=(j...  24.7 us
    unnamed x5, local copies, waits for them, and re-layouts  2.27 us
    another operation x3, other arithmetic, local(): jnp.stack([lax.dynamic_slice_in_dim(weight, mz * chunk, chunk), my_len.as...  2.1 us

profile of v1, /device:TPU:0, one launch (start us, length us, event | category | flops | bytes accessed | tf_op | source)
XLA Modules:
  0.0 96.3 jit_solution(12696478504928150962)
XLA Ops:
  0.7 0.7 convert_multiply_fusion.mix_w
  1.3 0.0 copy-start
  1.3 0.1 dynamic-slice_bitcast_fusion
  1.4 0.8 convert_bitcast_fusion
  2.2 0.7 compare_and_fusion
  2.8 1.3 %gather_fusion = s32[16]{0:T(128)S(1)} fusion(s32[512]{0:T(512)} %param.14, s32[1024]{0:T(1024)S(1)} %pad_clamp_fusion), kind=kCustom, calls=%fused_computation | custom fusion | bytes 192 | tf_op jit(solution)/shard_map/gather | solution.py:412
  4.2 1.3 %convert_bitcast_fusion.1 = (f32[16,1]{0,1:T(1,128)S(1)}, s32[16]{0:T(128)}) fusion(s32[16]{0:T(128)S(1)} %gather_fusion, s32[512]{0:T(512)} %param.14, s32[]{:T(128)S(6)} %select_n.43), kind=kLoop, calls=%fused_computation.27 | loop fusion | flops 32 | bytes 260 | tf_op jit(solution)/shard_map/stack | solution.py:413
  5.5 0.8 reshape.119
  6.3 0.7 copy.19.aux
  7.0 0.3 convert_reduce_fusion
  7.3 0.0 copy-start.1
  7.4 0.1 broadcast_add_fusion
  7.4 0.1 add.61
  7.5 0.7 select_reduce_fusion.send_idx
  8.2 0.7 select_reduce_fusion.1.send_code
  8.9 0.6 select_reduce_fusion.2.recv_idx
  9.5 1.8 %pad_maximum_fusion.wts = bf16[768,256]{1,0:T(8,128)(2,1)} fusion(bf16[256,256]{1,0:T(8,128)(2,1)} %param.18, bf16[256,256]{1,0:T(8,128)(2,1)} %param.17, bf16[64,256]{1,0:T(8,128)(2,1)} %param.16, bf16[192,256]{1,0:T(8,128)(2,1)} %bitcast.15), kind=kLoop, calls=%fused_computation.1 | loop fusion | flops 1572864 | bytes 786432 | tf_op jit(solution)/shard_map/concatenate | solution.py:422
  11.3 0.0 copy-done
  11.3 0.0 copy-done.1
  11.3 31.7 %shard_map.113 = (bf16[16,4,16,256]{3,2,1,0:T(8,128)(2,1)}, bf16[512,128]{1,0:T(8,128)(2,1)}, bf16[4,768,256]{2,1,0:T(8,128)(2,1)}) custom-call(s32[80]{0:T(128)} %select_reduce_fusion.send_idx, s32[64]{0:T(128)} %copy-done.1, f32[64]{0:T(128)} %copy-done, bf16[64,16,256]{2,1,0:T(8,128)(2,1)} %states.1, bf16[64,128]{1,0:T(8,128)(2,1)} %keys.1, ...), custom_call_target="tpu_custom_call" | custom-call | tf_op jit(solution)/shard_map/pallas_call | solution.py:429
  43.0 24.9 %shard_map.114 = (bf16[1024,256]{1,0:T(8,128)(2,1)}, f32[16,128]{1,0:T(8,128)}) custom-call(s32[16]{0:T(128)} %get-tuple-element.17.lens, bf16[1024,256]{1,0:T(8,128)(2,1)} %bitcast.13, bf16[4,768,256]{2,1,0:T(8,128)(2,1)} %get-tuple-element.10.wts, bf16[512,128]{1,0:T(8,128)(2,1)} %get-tuple-element.11.keys, bf16[256,128]{1,0:T(8,128)(2,1)} %w_proj.1, ...), custom_call_target="tpu_custom_call" | custom-call | tf_op jit(solution)/shard_map/pallas_call | solution.py:451
  68.0 24.7 %shard_map.115 = (f32[64,16,256]{2,1,0:T(8,128)}, f32[64,128]{1,0:T(8,128)}) custom-call(s32[80]{0:T(128)} %select_reduce_fusion.2.recv_idx, s32[64]{0:T(128)} %select_reduce_fusion.1.send_code, f32[64]{0:T(128)} %copy-done, bf16[16,4,16,256]{3,2,1,0:T(8,128)(2,1)} %bitcast.14, f32[16,128]{1,0:T(8,128)} %get-tuple-element.13.loss), custom_call_target="tpu_custom_call" | custom-call | tf_op jit(solution)/shard_map/pallas_call | solution.py:475
  92.7 1.4 %slice_reduce_fusion = f32[64]{0:T(128)} fusion(f32[64,128]{1,0:T(8,128)} %get-tuple-element.14), kind=kLoop, calls=%fused_computation.8 | loop fusion | bytes 512 | tf_op jit(solution)/shard_map/slice | solution.py:491
  94.1 2.3 %copy.21 = f32[64,16,256]{2,1,0:T(8,128)} copy(f32[64,16,256]{2,1,0:T(8,128)} %get-tuple-element.25) | data formatting | bytes 2097152
  (7 shorter events, 0.1 us)
Async XLA Ops:
  1.3 10.0 %copy-start = (f32[64]{0:T(128)}, f32[64]{0:T(128)S(1)}, u32[]{:S(2)}) copy-start(f32[64]{0:T(128)S(1)} %convert_multiply_fusion.mix_w) | copy-start | bytes 772
  7.3 4.0 %copy-start.1 = (s32[64]{0:T(128)}, s32[64]{0:T(128)S(1)}, u32[]{:S(2)}) copy-start(s32[64]{0:T(128)S(1)} %add_bitcast_fusion.recv_code) | copy-start | bytes 772

commit v2 on v1

--- a/solution.py
+++ b/solution.py
@@ -44,8 +44,8 @@
 
 def gather_kernel(
     n, mp, group, cap,
-    send_idx, recv_code, mix_w,
-    states, keys, wts,
+    send_idx, recv_code, mix_num,
+    states, keys, w_qkv, w_out, w_up, w_down,
     mixed, all_keys, all_wts,
     out_buf, in_buf, mix_buf,
     dp_s, dp_r, key_s, key_r, mp_s, mp_r, wz_s, wz_r, wg_s, wg_r,
@@ -53,7 +53,18 @@
     me, mz = lax.axis_index("dp"), lax.axis_index("mp")
     sessions = states.shape[0]
     chunk = sessions // mp
-    piece = wts.shape[0] // group
+    piece = all_wts.shape[1] // group
+    part_w = w_out.shape[0]
+    width = states.shape[2]
+    eye = (
+        lax.broadcasted_iota(jnp.int32, (part_w, part_w), 0)
+        == lax.broadcasted_iota(jnp.int32, (part_w, part_w), 1)
+    ).astype(F32).astype(BF16)
+    for j in range(3):
+        all_wts[mz, j * part_w : (j + 1) * part_w, :] = dot(eye, w_qkv[j], 1, 1).astype(BF16)
+    all_wts[mz, 3 * part_w : 4 * part_w, :] = w_out[...]
+    all_wts[mz, 4 * part_w : 4 * part_w + width, :] = w_up[...]
+    all_wts[mz, 4 * part_w + width :, :] = w_down[...]
     part = lax.rem(me, group)
     base = me - part
     rows = pl.ds(pl.multiple_of(part * piece, piece), piece)
@@ -67,7 +78,7 @@
     wz = []
     for o in range(1, mp):
         c = remote(
-            wts.at[rows], all_wts.at[mz, rows], wz_s.at[o], wz_r.at[o],
+            all_wts.at[mz, rows], all_wts.at[mz, rows], wz_s.at[o], wz_r.at[o],
             {"mp": lax.rem(mz + o, mp)},
         )
         c.start()
@@ -89,6 +100,25 @@
         c.start()
         pending.append(c)
     all_keys[pl.ds(pl.multiple_of(me * sessions, sessions), sessions), :] = keys[...]
+    for c in dp:
+        c.wait()
+
+    @pl.loop(0, sessions)
+    def _(i):
+        w = mix_num[i].astype(F32) * 0.0625
+        mix_buf[i] = (
+            w * states[i].astype(F32) + (1.0 - w) * in_buf[recv_code[i]].astype(F32)
+        ).astype(BF16)
+
+    for o in (2, 1, 3) if mp == 4 else range(1, mp):
+        peer = lax.rem(mz + o, mp)
+        c = remote(
+            mix_buf.at[pl.ds(peer * chunk, chunk)], mixed.at[pl.ds(0, chunk), mz],
+            mp_s.at[o], mp_r.at[o], {"mp": peer},
+        )
+        c.start()
+        pending.append(c)
+
     for o in range(1, mp):
         wz[o - 1].wait()
         held = lax.rem(mz + mp - o, mp)
@@ -99,25 +129,6 @@
             )
             c.start()
             pending.append(c)
-    all_wts[mz] = wts[...]
-    for c in dp:
-        c.wait()
-
-    @pl.loop(0, sessions)
-    def _(i):
-        w = mix_w[i]
-        mix_buf[i] = (
-            w * states[i].astype(F32) + (1.0 - w) * in_buf[recv_code[i]].astype(F32)
-        ).astype(BF16)
-
-    for o in (2, 1, 3) if mp == 4 else range(1, mp):
-        peer = lax.rem(mz + o, mp)
-        c = remote(
-            mix_buf.at[pl.ds(peer * chunk, chunk)], mixed.at[pl.ds(0, chunk), mz],
-            mp_s.at[o], mp_r.at[o], {"mp": peer},
-        )
-        c.start()
-        pending.append(c)
 
     @pl.loop(0, chunk)
     def _(i):
@@ -129,10 +140,10 @@
 
 def return_kernel(
     n, mp, cap,
-    recv_idx, send_code, mix_w,
+    recv_idx, mix_num,
     dmix, loss,
-    grad, all_loss,
-    dm_buf, ret_buf, arr_buf,
+    dm_buf, arr_buf, all_loss,
+    ret_buf,
     mp_s, mp_r, ls_s, ls_r, dp_s, dp_r,
 ):
     me, mz = lax.axis_index("dp"), lax.axis_index("mp")
@@ -163,7 +174,7 @@
     @pl.loop(0, n * cap)
     def _(j):
         i = recv_idx[j]
-        ret_buf[j] = ((1.0 - mix_w[i]) * dm_buf[i].astype(F32)).astype(BF16)
+        ret_buf[j] = ((1.0 - mix_num[i].astype(F32) * 0.0625) * dm_buf[i].astype(F32)).astype(BF16)
 
     back = []
     for o in range(1, n):
@@ -177,9 +188,21 @@
     for c in back:
         c.wait()
 
-    @pl.loop(0, sessions)
-    def _(s):
-        grad[s] = mix_w[s] * dm_buf[s].astype(F32) + arr_buf[send_code[s]].astype(F32)
+
+def final_kernel(send_code, mix_num, dm, arr, all_loss, grad, loss):
+    block = dm.shape[0]
+    sessions = all_loss.shape[0]
+    base = pl.program_id(0) * block
+    for j in range(block):
+        s = base + j
+        weight = mix_num[s].astype(F32) * 0.0625
+        grad[j] = weight * dm[j].astype(F32) + arr[send_code[s]].astype(F32)
+    diagonal = lax.broadcasted_iota(
+        jnp.int32, (sessions, sessions), 0
+    ) == lax.broadcasted_iota(jnp.int32, (sessions, sessions), 1)
+    loss[...] = jnp.sum(
+        jnp.where(diagonal, all_loss[:, 0:sessions], 0.0), axis=0, keepdims=True
+    )
 
 
 def dot(a, b, ca=1, cb=0, precision=None):
@@ -196,14 +219,26 @@
 
 def layer_kernel(
     events, heads, per_block,
-    lens,
-    mixed, wts, keys, w_proj, aux,
+    lengths, partner, mix_num,
+    mixed, wts, keys, w_proj,
     dmix, loss,
-    wqkv, w_out, proj, probs, slope, hpool, xpool, ctx, d_hid, d_ctx, g_row,
+    wqkv, w_out, proj, probs, slope, hpool, xpool, ctx, d_hid, d_ctx, g_row, aux, lens,
 ):
     mp = wts.shape[0]
     width = mixed.shape[1]
-    sessions = lens.shape[0]
+    sessions = hpool.shape[0]
+    first = lax.axis_index("mp") * sessions
+    start = lax.axis_index("dp") * (mp * sessions) + first
+    for i in range(sessions):
+        other = partner[start + i]
+        longest = jnp.maximum(lengths[start + i], lengths[other])
+        lens[i] = longest
+        row = slice(i, i + 1)
+        shape = (1, aux.shape[2])
+        aux[0, row, :] = jnp.full(shape, mix_num[first + i].astype(F32) * 0.0625, F32)
+        aux[1, row, :] = jnp.full(shape, longest.astype(F32), F32)
+        aux[2, row, :] = jnp.full(shape, (start + i).astype(F32), F32)
+        aux[3, row, :] = jnp.full(shape, other.astype(F32), F32)
     inner = heads * HD
     part = inner // mp
     ff_part = wts.shape[1] - 4 * part - width
@@ -259,7 +294,7 @@
         normed = unit.astype(BF16)
         qkv = dot(normed, wqkv[...], 1, 1).astype(BF16)
         proj[rows, :] = qkv
-        len_col = aux[srows, 1:2]
+        len_col = aux[1, srows, 0:1]
         pool_mask = jnp.where(
             (pool_lane // events == pool_row)
             & ((pool_lane % events).astype(F32) < len_col),
@@ -293,8 +328,8 @@
                 jnp.broadcast_to(seen, (8, lanes)), spread(v)
             )[0:1] / length.astype(F32)
 
-    weight, len_all = aux[:, 0:1], aux[:, 1:2]
-    own_id, partner_id = aux[:, 2:3], aux[:, 3:4]
+    weight, len_all = aux[0, :, 0:1], aux[1, :, 0:1]
+    own_id, partner_id = aux[2, :, 0:1], aux[3, :, 0:1]
     pooled = xpool[...] + dot_split(ctx[...], w_out[...])
     for m in range(mp):
         cols = slice(m * ff_part, (m + 1) * ff_part)
@@ -375,7 +410,6 @@
     cap = (sessions + n - 2) // (n - 1)
     slots = n * cap
     me = lax.axis_index("dp")
-    mz = lax.axis_index("mp")
     total = partner.shape[0]
     chunk = sessions // mp
     events = ev_part * mp
@@ -406,22 +440,6 @@
     recv_idx = jnp.sum(
         jnp.where(recv_code[None, :] == slot_ids[:, None], ids[None, :], 0), axis=1
     )
-    weight = mix_numer.astype(F32) / 16.0
-    start = me * sessions + mz * chunk
-    my_partner = lax.dynamic_slice_in_dim(partner, start, chunk)
-    my_len = jnp.maximum(lax.dynamic_slice_in_dim(lengths, start, chunk), lengths[my_partner])
-    aux = jnp.stack(
-        [
-            lax.dynamic_slice_in_dim(weight, mz * chunk, chunk),
-            my_len.astype(F32),
-            (start + jnp.arange(chunk, dtype=jnp.int32)).astype(F32),
-            my_partner.astype(F32),
-        ],
-        axis=1,
-    )
-    wts = jnp.concatenate(
-        [w_qkv.transpose(0, 2, 1).reshape(3 * inner_part, width), w_out, w_up, w_down], axis=0
-    )
     smem = pl.BlockSpec(memory_space=pltpu.SMEM)
     vmem = pl.BlockSpec(memory_space=pltpu.VMEM)
     dma = pltpu.SemaphoreType.DMA
@@ -431,9 +449,9 @@
         out_shape=(
             jax.ShapeDtypeStruct((chunk, mp, ev_part, width), BF16),
             jax.ShapeDtypeStruct((total, key_embed.shape[1]), BF16),
-            jax.ShapeDtypeStruct((mp,) + wts.shape, BF16),
+            jax.ShapeDtypeStruct((mp, 4 * inner_part + width + ff_part, width), BF16),
         ),
-        in_specs=[smem] * 3 + [vmem] * 3,
+        in_specs=[smem] * 3 + [vmem] * 6,
         out_specs=(vmem,) * 3,
         scratch_shapes=[
             pltpu.VMEM((slots, ev_part, width), BF16),
@@ -444,7 +462,7 @@
             dma((mp, group)), dma((mp, group)),
         ],
         compiler_params=pltpu.CompilerParams(collective_id=0, has_side_effects=True),
-    )(send_idx, recv_code, weight, states, key_embed, wts)
+    )(send_idx, recv_code, mix_numer, states, key_embed, w_qkv, w_out, w_up, w_down)
 
     rows = chunk * events
     per_block = min(8, chunk)
@@ -454,7 +472,7 @@
             jax.ShapeDtypeStruct((rows, width), BF16),
             jax.ShapeDtypeStruct((chunk, 128), F32),
         ),
-        in_specs=[smem] + [vmem] * 5,
+        in_specs=[smem] * 3 + [vmem] * 4,
         out_specs=(vmem, vmem),
         scratch_shapes=[
             pltpu.VMEM((3 * inner, width), BF16),
@@ -468,27 +486,49 @@
             pltpu.VMEM((chunk, mp * ff_part), F32),
             pltpu.VMEM((chunk, inner), F32),
             pltpu.VMEM((chunk, width), F32),
+            pltpu.VMEM((4, chunk, 128), F32),
+            pltpu.SMEM((chunk,), jnp.int32),
         ],
         compiler_params=pltpu.CompilerParams(vmem_limit_bytes=56 * 1024 * 1024),
-    )(my_len, mixed.reshape(rows, width), all_wts, all_keys, w_proj, aux)
-
-    grad, all_loss = pl.pallas_call(
+    )(lengths, partner, mix_numer, mixed.reshape(rows, width), all_wts, all_keys, w_proj)
+
+    dm_buf, arr_buf, all_loss = pl.pallas_call(
         functools.partial(return_kernel, n, mp, cap),
         out_shape=(
-            jax.ShapeDtypeStruct((sessions, ev_part, width), F32),
+            jax.ShapeDtypeStruct((sessions, ev_part, width), BF16),
+            jax.ShapeDtypeStruct((slots, ev_part, width), BF16),
             jax.ShapeDtypeStruct((sessions, 128), F32),
         ),
-        in_specs=[smem] * 3 + [vmem] * 2,
-        out_specs=(vmem, vmem),
+        in_specs=[smem] * 2 + [vmem] * 2,
+        out_specs=(vmem,) * 3,
         scratch_shapes=[
-            pltpu.VMEM((sessions, ev_part, width), BF16),
-            pltpu.VMEM((slots, ev_part, width), BF16),
             pltpu.VMEM((slots, ev_part, width), BF16),
             dma((mp,)), dma((mp,)), dma((mp,)), dma((mp,)), dma((n,)), dma((n,)),
         ],
         compiler_params=pltpu.CompilerParams(collective_id=1, has_side_effects=True),
-    )(recv_idx, send_code, weight, dmix.reshape(chunk, mp, ev_part, width), loss)
-    return (all_loss[:, 0], grad)
+    )(recv_idx, mix_numer, dmix.reshape(chunk, mp, ev_part, width), loss)
+
+    block = chunk
+    grad, loss_row = pl.pallas_call(
+        final_kernel,
+        grid=(sessions // block,),
+        out_shape=(
+            jax.ShapeDtypeStruct((sessions, ev_part, width), F32),
+            jax.ShapeDtypeStruct((1, sessions), F32),
+        ),
+        in_specs=[
+            smem,
+            smem,
+            pl.BlockSpec((block, ev_part, width), lambda b: (b, 0, 0)),
+            pl.BlockSpec((slots, ev_part, width), lambda b: (0, 0, 0)),
+            pl.BlockSpec((sessions, 128), lambda b: (0, 0)),
+        ],
+        out_specs=(
+            pl.BlockSpec((block, ev_part, width), lambda b: (b, 0, 0)),
+            pl.BlockSpec((1, sessions), lambda b: (0, 0)),
+        ),
+    )(send_code, mix_numer, dm_buf, arr_buf, all_loss)
+    return (loss_row.reshape(sessions), grad)
 
 
 def solution(mesh):

time: 98.1 us -> 94.5 us (0.963)
  Pallas kernels: 81.3 us -> 86.5 us
  other arithmetic: 7.71 us -> 3.13 us
  local copies, waits for them, and re-layouts: 6.58 us -> 2.54 us
    pallas_call x0 -> x1, Pallas kernels: none -> 3.61 us  [local(): pl.pallas_call(final_kernel, grid=(sessions // block,), out_shape=(jax.Sh...]
    another operation x3 -> x0, other arithmetic: 2.1 us -> none  [local(): jnp.stack([lax.dynamic_slice_in_dim(weight, mz * chunk, chunk), my_len.as...]
    pallas_call x1, Pallas kernels: 31.7 us -> 33.7 us  [local(): pl.pallas_call(functools.partial(gather_kernel, n, mp, group, cap), out_s...]
    concatenate x1 -> x0, other arithmetic: 1.81 us -> none  [local(): jnp.concatenate([w_qkv.transpose(0, 2, 1).reshape(3 * inner_part, width),...]
    slice x1 -> x0, local copies, waits for them, and re-layouts: 1.38 us -> none  [local(): return (all_loss[:, 0], grad)]
    gather x1 -> x0, local copies, waits for them, and re-layouts: 1.35 us -> none  [local(): lengths[my_partner]]
    unnamed x5 -> x3, local copies, waits for them, and re-layouts: 2.27 us -> 1.71 us
where the time goes in v2:
time: 94.5 us; the launch traced here: 92.9 us
  Pallas kernels  86.5 us (92%)
  other arithmetic  3.13 us (3%)
  local copies, waits for them, and re-layouts  2.54 us (3%)
    pallas_call x1, Pallas kernels, local(): pl.pallas_call(functools.partial(gather_kernel, n, mp, group, cap), out_s...  33.7 us
    pallas_call x1, Pallas kernels, local(): pl.pallas_call(functools.partial(layer_kernel, events, heads, per_block),...  25 us
    pallas_call x1, Pallas kernels, local(): pl.pallas_call(functools.partial(return_kernel, n, mp, cap), out_shape=(j...  24.2 us
    pallas_call x1, Pallas kernels, local(): pl.pallas_call(final_kernel, grid=(sessions // block,), out_shape=(jax.Sh...  3.61 us

profile of v2, /device:TPU:0, one launch (start us, length us, event | category | flops | bytes accessed | tf_op | source)
XLA Modules:
  0.0 92.9 jit_solution(13565598081968491969)
XLA Ops:
  0.6 0.7 compare_and_fusion
  1.3 0.8 reshape.109
  2.1 0.3 convert_reduce_fusion
  2.5 0.0 copy-start
  2.5 0.1 broadcast_add_fusion
  2.5 0.1 add.33
  2.6 0.7 select_reduce_fusion.send_idx
  3.3 0.7 select_reduce_fusion.1.send_code
  4.0 0.6 select_reduce_fusion.2.recv_idx
  4.6 1.7 %copy.13.w_qkv = bf16[3,256,64]{2,1,0:T(8,128)(2,1)} copy(bf16[3,256,64]{1,2,0:T(8,128)(2,1)} %param.15) | data formatting | bytes 196608 | tf_op args[5]
  6.3 0.0 copy-done
  6.3 33.7 %shard_map.113 = (bf16[16,4,16,256]{3,2,1,0:T(8,128)(2,1)}, bf16[512,128]{1,0:T(8,128)(2,1)}, bf16[4,768,256]{2,1,0:T(8,128)(2,1)}) custom-call(s32[80]{0:T(128)} %select_reduce_fusion.send_idx, s32[64]{0:T(128)} %copy-done, s32[64]{0:T(128)} %mix_num.7, bf16[64,16,256]{2,1,0:T(8,128)(2,1)} %states.1, bf16[64,128]{1,0:T(8,128)(2,1)} %keys.1, ...), custom_call_target="tpu_custom_call" | custom-call | tf_op jit(solution)/shard_map/pallas_call | solution.py:447
  40.1 25.0 %shard_map.114 = (bf16[1024,256]{1,0:T(8,128)(2,1)}, f32[16,128]{1,0:T(8,128)}) custom-call(s32[512]{0:T(512)} %lengths.1, s32[512]{0:T(512)} %partner.1, s32[64]{0:T(128)} %mix_num.7, bf16[1024,256]{1,0:T(8,128)(2,1)} %bitcast.5, bf16[4,768,256]{2,1,0:T(8,128)(2,1)} %get-tuple-element.13.wts, bf16[512,128]{1,0:T(8,128)(2,1)} %get-tuple-element.14.keys, ...), custom_call_target="tpu_custom_call" | custom-call | tf_op jit(solution)/shard_map/pallas_call | solution.py:469
  65.0 24.2 %shard_map.115 = (bf16[64,16,256]{2,1,0:T(8,128)(2,1)}, bf16[80,16,256]{2,1,0:T(8,128)(2,1)}, f32[64,128]{1,0:T(8,128)}) custom-call(s32[80]{0:T(128)} %select_reduce_fusion.2.recv_idx, s32[64]{0:T(128)} %mix_num.7, bf16[16,4,16,256]{3,2,1,0:T(8,128)(2,1)} %bitcast.6, f32[16,128]{1,0:T(8,128)} %get-tuple-element.16.loss), custom_call_target="tpu_custom_call" | custom-call | tf_op jit(solution)/shard_map/pallas_call | solution.py:495
  89.3 3.6 %shard_map.116 = (f32[64,16,256]{2,1,0:T(8,128)}, f32[1,64]{1,0:T(1,128)}) custom-call(s32[64]{0:T(128)} %select_reduce_fusion.1.send_code, s32[64]{0:T(128)} %mix_num.7, bf16[64,16,256]{2,1,0:T(8,128)(2,1)} %get-tuple-element.17.dm, bf16[80,16,256]{2,1,0:T(8,128)(2,1)} %get-tuple-element.18.arr, f32[64,128]{1,0:T(8,128)} %get-tuple-element.19.all_loss), custom_call_target="tpu_custom_call" | custom-call | tf_op jit(solution)/shard_map/pallas_call | solution.py:512
  (4 shorter events, 0.0 us)
Async XLA Ops:
  2.5 3.9 %copy-start = (s32[64]{0:T(128)}, s32[64]{0:T(128)S(1)}, u32[]{:S(2)}) copy-start(s32[64]{0:T(128)S(1)} %add_bitcast_fusion.recv_code) | copy-start | bytes 772

commit v3 on v2

--- a/solution.py
+++ b/solution.py
@@ -47,33 +47,37 @@
     send_idx, recv_code, mix_num,
     states, keys, w_qkv, w_out, w_up, w_down,
     mixed, all_keys, all_wts,
-    out_buf, in_buf, mix_buf,
-    dp_s, dp_r, key_s, key_r, mp_s, mp_r, wz_s, wz_r, wg_s, wg_r,
+    out_buf, in_lo, in_hi, mix_buf,
+    dp_s, dp_r, key_s, key_r, mp_s, mp_r, wz_s, wz_r, wg_s, wg_r, wc_s, wc_r,
 ):
     me, mz = lax.axis_index("dp"), lax.axis_index("mp")
+    in_buf = (in_lo, in_hi)
     sessions = states.shape[0]
+    half = out_buf.shape[3]
     chunk = sessions // mp
+    chips = group // 2
     piece = all_wts.shape[1] // group
     part_w = w_out.shape[0]
     width = states.shape[2]
-    eye = (
-        lax.broadcasted_iota(jnp.int32, (part_w, part_w), 0)
-        == lax.broadcasted_iota(jnp.int32, (part_w, part_w), 1)
-    ).astype(F32).astype(BF16)
     for j in range(3):
-        all_wts[mz, j * part_w : (j + 1) * part_w, :] = dot(eye, w_qkv[j], 1, 1).astype(BF16)
+        all_wts[mz, j * part_w : (j + 1) * part_w, :] = w_qkv[j]
     all_wts[mz, 3 * part_w : 4 * part_w, :] = w_out[...]
     all_wts[mz, 4 * part_w : 4 * part_w + width, :] = w_up[...]
     all_wts[mz, 4 * part_w + width :, :] = w_down[...]
-    part = lax.rem(me, group)
-    base = me - part
-    rows = pl.ds(pl.multiple_of(part * piece, piece), piece)
-    greet(n, mp)
+    place = lax.rem(me, group)
+    base = me - place
+    core = lax.rem(place, 2)
+    chip = place // 2
+    core_rows = pl.ds(pl.multiple_of(core * (chips * piece), piece), chips * piece)
+    rows = pl.ds(pl.multiple_of((core * chips + chip) * piece, piece), piece)
 
     @pl.loop(0, n * cap)
     def _(j):
-        out_buf[j] = states[send_idx[j]]
-
+        i = send_idx[j]
+        for h in range(2):
+            out_buf[h, j] = states[i, :, h * half : (h + 1) * half]
+
+    greet(n, mp)
     pending = []
     wz = []
     for o in range(1, mp):
@@ -83,57 +87,74 @@
         )
         c.start()
         wz.append(c)
-    dp = []
-    for o in range(1, n):
-        peer = lax.rem(me + o, n)
-        c = remote(
-            out_buf.at[pl.ds(peer * cap, cap)], in_buf.at[pl.ds(me * cap, cap)],
-            dp_s.at[o], dp_r.at[o], {"dp": peer},
-        )
-        c.start()
-        dp.append(c)
+    dp = [[], []]
+    for h in range(2):
+        for o in range(1, n):
+            peer = lax.rem(me + o, n)
+            c = remote(
+                out_buf.at[h, pl.ds(peer * cap, cap)], in_buf[h].at[pl.ds(me * cap, cap)],
+                dp_s.at[h, o], dp_r.at[h, o], {"dp": peer},
+            )
+            c.start()
+            dp[h].append(c)
+    key_rows = pl.ds(pl.multiple_of(me * sessions, sessions), sessions)
     for o in range(1, n):
         c = remote(
-            keys, all_keys.at[pl.ds(pl.multiple_of(me * sessions, sessions), sessions)],
-            key_s.at[o], key_r.at[o], {"dp": lax.rem(me + o, n)},
+            keys, all_keys.at[key_rows], key_s.at[o], key_r.at[o], {"dp": lax.rem(me + o, n)}
         )
         c.start()
         pending.append(c)
-    all_keys[pl.ds(pl.multiple_of(me * sessions, sessions), sessions), :] = keys[...]
-    for c in dp:
-        c.wait()
-
-    @pl.loop(0, sessions)
-    def _(i):
-        w = mix_num[i].astype(F32) * 0.0625
-        mix_buf[i] = (
-            w * states[i].astype(F32) + (1.0 - w) * in_buf[recv_code[i]].astype(F32)
-        ).astype(BF16)
-
-    for o in (2, 1, 3) if mp == 4 else range(1, mp):
-        peer = lax.rem(mz + o, mp)
-        c = remote(
-            mix_buf.at[pl.ds(peer * chunk, chunk)], mixed.at[pl.ds(0, chunk), mz],
-            mp_s.at[o], mp_r.at[o], {"mp": peer},
-        )
-        c.start()
-        pending.append(c)
-
-    for o in range(1, mp):
-        wz[o - 1].wait()
-        held = lax.rem(mz + mp - o, mp)
-        for g in range(1, group):
+    all_keys[key_rows, :] = keys[...]
+    plane = []
+    for h in range(2):
+        cols = slice(h * half, (h + 1) * half)
+        for c in dp[h]:
+            c.wait()
+
+        @pl.loop(0, sessions)
+        def _(i):
+            w = mix_num[i].astype(F32) * 0.0625
+            mix_buf[h, i] = (
+                w * states[i, :, cols].astype(F32)
+                + (1.0 - w) * in_buf[h][recv_code[i]].astype(F32)
+            ).astype(BF16)
+
+        for o in (2, 1, 3) if mp == 4 else range(1, mp):
+            peer = lax.rem(mz + o, mp)
             c = remote(
-                all_wts.at[held, rows], all_wts.at[held, rows],
-                wg_s.at[o, g], wg_r.at[o, g], {"dp": base + lax.rem(part + g, group)},
+                mix_buf.at[h, pl.ds(peer * chunk, chunk)],
+                mixed.at[pl.ds(0, chunk), mz, :, cols],
+                mp_s.at[h, o], mp_r.at[h, o], {"mp": peer},
             )
             c.start()
             pending.append(c)
-
-    @pl.loop(0, chunk)
-    def _(i):
-        mixed[i, mz] = mix_buf[mz * chunk + i]
-
+        if h == 0:
+            for o in range(1, mp):
+                wz[o - 1].wait()
+                held = lax.rem(mz + mp - o, mp)
+                for g in range(1, chips):
+                    peer = base + lax.rem(chip + g, chips) * 2 + core
+                    c = remote(
+                        all_wts.at[held, rows], all_wts.at[held, rows],
+                        wg_s.at[o, g], wg_r.at[o, g], {"dp": peer},
+                    )
+                    c.start()
+                    plane.append(c)
+
+        @pl.loop(0, chunk)
+        def _(i):
+            mixed[i, mz, :, cols] = mix_buf[h, mz * chunk + i]
+
+    for c in plane:
+        c.wait()
+    for o in range(1, mp):
+        held = lax.rem(mz + mp - o, mp)
+        c = remote(
+            all_wts.at[held, core_rows], all_wts.at[held, core_rows],
+            wc_s.at[o], wc_r.at[o], {"dp": me + 1 - 2 * core},
+        )
+        c.start()
+        pending.append(c)
     for c in pending:
         c.wait()
 
@@ -142,61 +163,76 @@
     n, mp, cap,
     recv_idx, mix_num,
     dmix, loss,
-    dm_buf, arr_buf, all_loss,
+    dm_lo, dm_hi, arr_buf, all_loss,
     ret_buf,
     mp_s, mp_r, ls_s, ls_r, dp_s, dp_r,
 ):
     me, mz = lax.axis_index("dp"), lax.axis_index("mp")
     chunk = dmix.shape[0]
-    sessions = dm_buf.shape[0]
+    dm_buf = (dm_lo, dm_hi)
+    half = dm_lo.shape[2]
     greet(n, mp)
     mine = pl.ds(pl.multiple_of(mz * chunk, chunk), chunk)
-    first = []
-    for o in (2, 1, 3) if mp == 4 else range(1, mp):
-        peer = lax.rem(mz + o, mp)
+    first = [[], []]
+    pending = []
+    for h in range(2):
+        for o in (2, 1, 3) if mp == 4 else range(1, mp):
+            peer = lax.rem(mz + o, mp)
+            c = remote(
+                dmix.at[pl.ds(0, chunk), peer, :, h * half : (h + 1) * half],
+                dm_buf[h].at[mine],
+                mp_s.at[h, o], mp_r.at[h, o], {"mp": peer},
+            )
+            c.start()
+            first[h].append(c)
+    for o in range(1, mp):
         c = remote(
-            dmix.at[pl.ds(0, chunk), peer], dm_buf.at[mine], mp_s.at[o], mp_r.at[o], {"mp": peer}
+            loss, all_loss.at[mine], ls_s.at[o], ls_r.at[o], {"mp": lax.rem(mz + o, mp)}
         )
         c.start()
-        first.append(c)
-        c = remote(loss, all_loss.at[mine], ls_s.at[o], ls_r.at[o], {"mp": peer})
-        c.start()
-        first.append(c)
+        pending.append(c)
     all_loss[mine, :] = loss[...]
 
     @pl.loop(0, chunk)
     def _(i):
-        dm_buf[mz * chunk + i] = dmix[i, mz]
-
-    for c in first:
+        for h in range(2):
+            dm_buf[h][mz * chunk + i] = dmix[i, mz, :, h * half : (h + 1) * half]
+
+    for h in range(2):
+        for c in first[h]:
+            c.wait()
+
+        @pl.loop(0, n * cap)
+        def _(j):
+            i = recv_idx[j]
+            ret_buf[h, j] = (
+                (1.0 - mix_num[i].astype(F32) * 0.0625) * dm_buf[h][i].astype(F32)
+            ).astype(BF16)
+
+        for o in range(1, n):
+            peer = lax.rem(me + o, n)
+            c = remote(
+                ret_buf.at[h, pl.ds(peer * cap, cap)], arr_buf.at[h, pl.ds(me * cap, cap)],
+                dp_s.at[h, o], dp_r.at[h, o], {"dp": peer},
+            )
+            c.start()
+            pending.append(c)
+    for c in pending:
         c.wait()
 
-    @pl.loop(0, n * cap)
-    def _(j):
-        i = recv_idx[j]
-        ret_buf[j] = ((1.0 - mix_num[i].astype(F32) * 0.0625) * dm_buf[i].astype(F32)).astype(BF16)
-
-    back = []
-    for o in range(1, n):
-        peer = lax.rem(me + o, n)
-        c = remote(
-            ret_buf.at[pl.ds(peer * cap, cap)], arr_buf.at[pl.ds(me * cap, cap)],
-            dp_s.at[o], dp_r.at[o], {"dp": peer},
-        )
-        c.start()
-        back.append(c)
-    for c in back:
-        c.wait()
-
-
-def final_kernel(send_code, mix_num, dm, arr, all_loss, grad, loss):
-    block = dm.shape[0]
+
+def final_kernel(send_code, mix_num, dm_lo, dm_hi, arr, all_loss, grad, loss):
+    dm = (dm_lo, dm_hi)
+    block, half = dm_lo.shape[0], dm_lo.shape[2]
     sessions = all_loss.shape[0]
     base = pl.program_id(0) * block
     for j in range(block):
         s = base + j
         weight = mix_num[s].astype(F32) * 0.0625
-        grad[j] = weight * dm[j].astype(F32) + arr[send_code[s]].astype(F32)
+        for h in range(2):
+            grad[j, :, h * half : (h + 1) * half] = (
+                weight * dm[h][j].astype(F32) + arr[h, send_code[s]].astype(F32)
+            )
     diagonal = lax.broadcasted_iota(
         jnp.int32, (sessions, sessions), 0
     ) == lax.broadcasted_iota(jnp.int32, (sessions, sessions), 1)
@@ -417,7 +453,8 @@
     inner = inner_part * mp
     heads = inner // HD
     ff_part = w_up.shape[1]
-    group = 8 if n % 8 == 0 else 1
+    group = 8 if n % 8 == 0 else 2
+    half = width // 2
 
     source = partner.reshape(n, sessions) // sessions
     ids = jnp.arange(sessions, dtype=jnp.int32)
@@ -454,15 +491,16 @@
         in_specs=[smem] * 3 + [vmem] * 6,
         out_specs=(vmem,) * 3,
         scratch_shapes=[
-            pltpu.VMEM((slots, ev_part, width), BF16),
-            pltpu.VMEM((slots, ev_part, width), BF16),
-            pltpu.VMEM((sessions, ev_part, width), BF16),
-            dma((n,)), dma((n,)), dma((n,)), dma((n,)),
-            dma((mp,)), dma((mp,)), dma((mp,)), dma((mp,)),
-            dma((mp, group)), dma((mp, group)),
+            pltpu.VMEM((2, slots, ev_part, half), BF16),
+            pltpu.VMEM((slots, ev_part, half), BF16),
+            pltpu.VMEM((slots, ev_part, half), BF16),
+            pltpu.VMEM((2, sessions, ev_part, half), BF16),
+            dma((2, n)), dma((2, n)), dma((n,)), dma((n,)),
+            dma((2, mp)), dma((2, mp)), dma((mp,)), dma((mp,)),
+            dma((mp, group)), dma((mp, group)), dma((mp,)), dma((mp,)),
         ],
         compiler_params=pltpu.CompilerParams(collective_id=0, has_side_effects=True),
-    )(send_idx, recv_code, mix_numer, states, key_embed, w_qkv, w_out, w_up, w_down)
+    )(send_idx, recv_code, mix_numer, states, key_embed, w_qkv.transpose(0, 2, 1), w_out, w_up, w_down)
 
     rows = chunk * events
     per_block = min(8, chunk)
@@ -492,18 +530,19 @@
         compiler_params=pltpu.CompilerParams(vmem_limit_bytes=56 * 1024 * 1024),
     )(lengths, partner, mix_numer, mixed.reshape(rows, width), all_wts, all_keys, w_proj)
 
-    dm_buf, arr_buf, all_loss = pl.pallas_call(
+    dm_lo, dm_hi, arr_buf, all_loss = pl.pallas_call(
         functools.partial(return_kernel, n, mp, cap),
         out_shape=(
-            jax.ShapeDtypeStruct((sessions, ev_part, width), BF16),
-            jax.ShapeDtypeStruct((slots, ev_part, width), BF16),
+            jax.ShapeDtypeStruct((sessions, ev_part, half), BF16),
+            jax.ShapeDtypeStruct((sessions, ev_part, half), BF16),
+            jax.ShapeDtypeStruct((2, slots, ev_part, half), BF16),
             jax.ShapeDtypeStruct((sessions, 128), F32),
         ),
         in_specs=[smem] * 2 + [vmem] * 2,
-        out_specs=(vmem,) * 3,
+        out_specs=(vmem,) * 4,
         scratch_shapes=[
-            pltpu.VMEM((slots, ev_part, width), BF16),
-            dma((mp,)), dma((mp,)), dma((mp,)), dma((mp,)), dma((n,)), dma((n,)),
+            pltpu.VMEM((2, slots, ev_part, half), BF16),
+            dma((2, mp)), dma((2, mp)), dma((mp,)), dma((mp,)), dma((2, n)), dma((2, n)),
         ],
         compiler_params=pltpu.CompilerParams(collective_id=1, has_side_effects=True),
     )(recv_idx, mix_numer, dmix.reshape(chunk, mp, ev_part, width), loss)
@@ -519,15 +558,16 @@
         in_specs=[
             smem,
             smem,
-            pl.BlockSpec((block, ev_part, width), lambda b: (b, 0, 0)),
-            pl.BlockSpec((slots, ev_part, width), lambda b: (0, 0, 0)),
+            pl.BlockSpec((block, ev_part, half), lambda b: (b, 0, 0)),
+            pl.BlockSpec((block, ev_part, half), lambda b: (b, 0, 0)),
+            pl.BlockSpec((2, slots, ev_part, half), lambda b: (0, 0, 0, 0)),
             pl.BlockSpec((sessions, 128), lambda b: (0, 0)),
         ],
         out_specs=(
             pl.BlockSpec((block, ev_part, width), lambda b: (b, 0, 0)),
             pl.BlockSpec((1, sessions), lambda b: (0, 0)),
         ),
-    )(send_code, mix_numer, dm_buf, arr_buf, all_loss)
+    )(send_code, mix_numer, dm_lo, dm_hi, arr_buf, all_loss)
     return (loss_row.reshape(sessions), grad)
 
 

time: 94.5 us -> 85.6 us (0.906); the launches traced: 92.9 us -> 85.2 us
  Pallas kernels: 86.5 us -> 80.6 us
  local copies, waits for them, and re-layouts: 2.54 us -> 0.84 us
    pallas_call x1, Pallas kernels: 33.7 us -> 28.3 us  [local(): pl.pallas_call(functools.partial(gather_kernel, n, mp, group, cap), out_s...]
    unnamed x3 -> x2, local copies, waits for them, and re-layouts: 1.71 us -> 0.01 us
where the time goes in v3:
time: 85.6 us; the launch traced here: 85.2 us
  Pallas kernels  80.6 us (94%)
  other arithmetic  3.06 us (4%)
    pallas_call x1, Pallas kernels, local(): pl.pallas_call(functools.partial(gather_kernel, n, mp, group, cap), out_s...  28.3 us
    pallas_call x1, Pallas kernels, local(): pl.pallas_call(functools.partial(layer_kernel, events, heads, per_block),...  25 us
    pallas_call x1, Pallas kernels, local(): pl.pallas_call(functools.partial(return_kernel, n, mp, cap), out_shape=(j...  23.8 us
    pallas_call x1, Pallas kernels, local(): pl.pallas_call(final_kernel, grid=(sessions // block,), out_shape=(jax.Sh...  3.63 us

profile of v3, /device:TPU:0, one launch (start us, length us, event | category | flops | bytes accessed | tf_op | source)
XLA Modules:
  0.0 85.2 jit_solution(5451268645216006684)
XLA Ops:
  0.6 0.7 compare_and_fusion
  1.3 0.8 reshape.109
  2.1 0.3 convert_reduce_fusion
  2.5 0.0 copy-start
  2.5 0.1 broadcast_add_fusion
  2.5 0.1 add.33
  2.6 0.6 select_reduce_fusion.send_idx
  3.3 0.7 select_reduce_fusion.1.send_code
  4.0 0.6 select_reduce_fusion.2.recv_idx
  4.6 0.0 copy-done
  4.6 28.3 %shard_map.113 = (bf16[16,4,16,256]{3,2,1,0:T(8,128)(2,1)}, bf16[512,128]{1,0:T(8,128)(2,1)}, bf16[4,768,256]{2,1,0:T(8,128)(2,1)}) custom-call(s32[80]{0:T(128)} %select_reduce_fusion.send_idx, s32[64]{0:T(128)} %copy-done, s32[64]{0:T(128)} %mix_num.7, bf16[64,16,256]{2,1,0:T(8,128)(2,1)} %states.1, bf16[64,128]{1,0:T(8,128)(2,1)} %keys.1, ...), custom_call_target="tpu_custom_call" | custom-call | tf_op jit(solution)/shard_map/pallas_call | solution.py:484
  32.8 25.0 %shard_map.114 = (bf16[1024,256]{1,0:T(8,128)(2,1)}, f32[16,128]{1,0:T(8,128)}) custom-call(s32[512]{0:T(512)} %lengths.1, s32[512]{0:T(512)} %partner.1, s32[64]{0:T(128)} %mix_num.7, bf16[1024,256]{1,0:T(8,128)(2,1)} %bitcast.6, bf16[4,768,256]{2,1,0:T(8,128)(2,1)} %get-tuple-element.14.wts, bf16[512,128]{1,0:T(8,128)(2,1)} %get-tuple-element.15.keys, ...), custom_call_target="tpu_custom_call" | custom-call | tf_op jit(solution)/shard_map/pallas_call | solution.py:507
  57.8 23.8 %shard_map.115 = (bf16[64,16,128]{2,1,0:T(8,128)(2,1)}, bf16[64,16,128]{2,1,0:T(8,128)(2,1)}, bf16[2,80,16,128]{3,2,1,0:T(8,128)(2,1)}, f32[64,128]{1,0:T(8,128)}) custom-call(s32[80]{0:T(128)} %select_reduce_fusion.2.recv_idx, s32[64]{0:T(128)} %mix_num.7, bf16[16,4,16,256]{3,2,1,0:T(8,128)(2,1)} %bitcast.7, f32[16,128]{1,0:T(8,128)} %get-tuple-element.17.loss), custom_call_target="tpu_custom_call" | custom-call | tf_op jit(solution)/shard_map/pallas_call | solution.py:533
  81.6 3.6 %shard_map.116 = (f32[64,16,256]{2,1,0:T(8,128)}, f32[1,64]{1,0:T(1,128)}) custom-call(s32[64]{0:T(128)} %select_reduce_fusion.1.send_code, s32[64]{0:T(128)} %mix_num.7, bf16[64,16,128]{2,1,0:T(8,128)(2,1)} %get-tuple-element.18.dm_lo, bf16[64,16,128]{2,1,0:T(8,128)(2,1)} %get-tuple-element.19.dm_hi, bf16[2,80,16,128]{3,2,1,0:T(8,128)(2,1)} %get-tuple-element.20.arr, ...), custom_call_target="tpu_custom_call" | custom-call | tf_op jit(solution)/shard_map/pallas_call | solution.py:551
  (4 shorter events, 0.0 us)
Async XLA Ops:
  2.5 2.1 %copy-start = (s32[64]{0:T(128)}, s32[64]{0:T(128)S(1)}, u32[]{:S(2)}) copy-start(s32[64]{0:T(128)S(1)} %add_bitcast_fusion.recv_code) | copy-start | bytes 772

commit v4 on v3

--- a/solution.py
+++ b/solution.py
@@ -71,7 +71,7 @@
     core_rows = pl.ds(pl.multiple_of(core * (chips * piece), piece), chips * piece)
     rows = pl.ds(pl.multiple_of((core * chips + chip) * piece, piece), piece)
 
-    @pl.loop(0, n * cap)
+    @pl.loop(0, n * cap, unroll=8)
     def _(j):
         i = send_idx[j]
         for h in range(2):
@@ -111,7 +111,7 @@
         for c in dp[h]:
             c.wait()
 
-        @pl.loop(0, sessions)
+        @pl.loop(0, sessions, unroll=8)
         def _(i):
             w = mix_num[i].astype(F32) * 0.0625
             mix_buf[h, i] = (
@@ -141,7 +141,7 @@
                     c.start()
                     plane.append(c)
 
-        @pl.loop(0, chunk)
+        @pl.loop(0, chunk, unroll=8)
         def _(i):
             mixed[i, mz, :, cols] = mix_buf[h, mz * chunk + i]
 
@@ -193,7 +193,7 @@
         pending.append(c)
     all_loss[mine, :] = loss[...]
 
-    @pl.loop(0, chunk)
+    @pl.loop(0, chunk, unroll=8)
     def _(i):
         for h in range(2):
             dm_buf[h][mz * chunk + i] = dmix[i, mz, :, h * half : (h + 1) * half]
@@ -202,7 +202,7 @@
         for c in first[h]:
             c.wait()
 
-        @pl.loop(0, n * cap)
+        @pl.loop(0, n * cap, unroll=8)
         def _(j):
             i = recv_idx[j]
             ret_buf[h, j] = (

time: 85.6 us -> 83.9 us (0.980)
  Pallas kernels: 80.6 us -> 78.9 us
    pallas_call x1, Pallas kernels: 23.8 us -> 22.4 us  [local(): pl.pallas_call(functools.partial(return_kernel, n, mp, cap), out_shape=(j...]
where the time goes in v4:
time: 83.9 us; the launch traced here: 83.5 us
  Pallas kernels  78.9 us (94%)
  other arithmetic  3.06 us (4%)
  local copies, waits for them, and re-layouts  0.84 us (1%)
    pallas_call x1, Pallas kernels, local(): pl.pallas_call(functools.partial(gather_kernel, n, mp, group, cap), out_s...  28 us
    pallas_call x1, Pallas kernels, local(): pl.pallas_call(functools.partial(layer_kernel, events, heads, per_block),...  25 us
    pallas_call x1, Pallas kernels, local(): pl.pallas_call(functools.partial(return_kernel, n, mp, cap), out_shape=(j...  22.4 us
    pallas_call x1, Pallas kernels, local(): pl.pallas_call(final_kernel, grid=(sessions // block,), out_shape=(jax.Sh...  3.63 us

profile of v4, /device:TPU:0, one launch (start us, length us, event | category | flops | bytes accessed | tf_op | source)
XLA Modules:
  0.0 83.5 jit_solution(5312584509532553897)
XLA Ops:
  0.6 0.7 compare_and_fusion
  1.3 0.8 reshape.109
  2.1 0.3 convert_reduce_fusion
  2.5 0.0 copy-start
  2.5 0.1 broadcast_add_fusion
  2.5 0.1 add.33
  2.6 0.6 select_reduce_fusion.send_idx
  3.3 0.7 select_reduce_fusion.1.send_code
  4.0 0.6 select_reduce_fusion.2.recv_idx
  4.6 0.0 copy-done
  4.6 28.0 %shard_map.113 = (bf16[16,4,16,256]{3,2,1,0:T(8,128)(2,1)}, bf16[512,128]{1,0:T(8,128)(2,1)}, bf16[4,768,256]{2,1,0:T(8,128)(2,1)}) custom-call(s32[80]{0:T(128)} %select_reduce_fusion.send_idx, s32[64]{0:T(128)} %copy-done, s32[64]{0:T(128)} %mix_num.7, bf16[64,16,256]{2,1,0:T(8,128)(2,1)} %states.1, bf16[64,128]{1,0:T(8,128)(2,1)} %keys.1, ...), custom_call_target="tpu_custom_call" | custom-call | tf_op jit(solution)/shard_map/pallas_call | solution.py:484
  32.5 25.0 %shard_map.114 = (bf16[1024,256]{1,0:T(8,128)(2,1)}, f32[16,128]{1,0:T(8,128)}) custom-call(s32[512]{0:T(512)} %lengths.1, s32[512]{0:T(512)} %partner.1, s32[64]{0:T(128)} %mix_num.7, bf16[1024,256]{1,0:T(8,128)(2,1)} %bitcast.6, bf16[4,768,256]{2,1,0:T(8,128)(2,1)} %get-tuple-element.14.wts, bf16[512,128]{1,0:T(8,128)(2,1)} %get-tuple-element.15.keys, ...), custom_call_target="tpu_custom_call" | custom-call | tf_op jit(solution)/shard_map/pallas_call | solution.py:507
  57.5 22.4 %shard_map.115 = (bf16[64,16,128]{2,1,0:T(8,128)(2,1)}, bf16[64,16,128]{2,1,0:T(8,128)(2,1)}, bf16[2,80,16,128]{3,2,1,0:T(8,128)(2,1)}, f32[64,128]{1,0:T(8,128)}) custom-call(s32[80]{0:T(128)} %select_reduce_fusion.2.recv_idx, s32[64]{0:T(128)} %mix_num.7, bf16[16,4,16,256]{3,2,1,0:T(8,128)(2,1)} %bitcast.7, f32[16,128]{1,0:T(8,128)} %get-tuple-element.17.loss), custom_call_target="tpu_custom_call" | custom-call | tf_op jit(solution)/shard_map/pallas_call | solution.py:533
  79.9 3.6 %shard_map.116 = (f32[64,16,256]{2,1,0:T(8,128)}, f32[1,64]{1,0:T(1,128)}) custom-call(s32[64]{0:T(128)} %select_reduce_fusion.1.send_code, s32[64]{0:T(128)} %mix_num.7, bf16[64,16,128]{2,1,0:T(8,128)(2,1)} %get-tuple-element.18.dm_lo, bf16[64,16,128]{2,1,0:T(8,128)(2,1)} %get-tuple-element.19.dm_hi, bf16[2,80,16,128]{3,2,1,0:T(8,128)(2,1)} %get-tuple-element.20.arr, ...), custom_call_target="tpu_custom_call" | custom-call | tf_op jit(solution)/shard_map/pallas_call | solution.py:551
  (4 shorter events, 0.0 us)
Async XLA Ops:
  2.5 2.1 %copy-start = (s32[64]{0:T(128)}, s32[64]{0:T(128)S(1)}, u32[]{:S(2)}) copy-start(s32[64]{0:T(128)S(1)} %add_bitcast_fusion.recv_code) | copy-start | bytes 772
